TPU v7x, 512 devices: a whole 4x8x8 slice. The times are simulated.
512 devices in a mesh: row: 16 (over y, z_lo), col: 32 (over z_hi, x, core).
Axes of the slice: x: 4, y: 8, z: 8 (z_hi: 4, z_lo: 2; z = z_hi * 2 + z_lo), core: 2. Of those that a mesh axis runs over, the one named last changes fastest.
Arguments:
- amplitudes: bfloat16 [16384, 16384], P('row', 'col'), may hold values from -6 to 6
- df_factors: bfloat16 [16384, 1024], P('col', 'row'), may hold values from -0.375 to 0.375
- ladder: bfloat16 [1024, 1024], P(('row', 'col')), may hold values from -0.1875 to 0.1875
- occ_energy: float32 [200], replicated, may hold values from -2.5 to -0.3
- occ_index: int32 [32], replicated, may hold values from 0 to 199
- vir_energy: float32 [512], replicated, may hold values from 0.3 to 3
- vir_map: int32 [512], replicated, may hold values from 0 to 511, each once
Outputs:
- residual_update: bfloat16 [16384, 16384], P('row', 'col')
All inputs are finite; a program needn't handle non-finite values.
Results may differ from a plain program's by a relative error of at most 0.0045.
The roundings to bfloat16 on the way count: a program that leaves them out, or rounds other values in their place, can miss the bound.
Values may be sent and summed in bfloat16 or wider, within the bound.
No kernel may reach another device: no remote copies, remote signals or barrier semaphores. Data moves between devices by JAX's collectives and lax.ppermute only.
A program may use at most 64 MiB of HBM per device.

v0:
```python
import jax
import jax.numpy as jnp
from jax import lax
from jax.sharding import PartitionSpec as P

VIR = 512


def joined_along(tiles, dim):
    tiles = jnp.moveaxis(tiles, 0, dim)
    dims = tiles.shape
    return tiles.reshape(*dims[:dim], dims[dim] * dims[dim + 1], *dims[dim + 2 :])


def from_everyone(value, axis):
    devices = lax.axis_size(axis)
    return lax.all_to_all(
        jnp.broadcast_to(value[None], (devices, *value.shape)), axis, 0, 0, tiled=True
    )


def gather_directly(value, axis, dim):
    return joined_along(from_everyone(value, axis), dim)


def split_up(value, dim, devices):
    dims = value.shape
    tiles = value.reshape(*dims[:dim], devices, dims[dim] // devices, *dims[dim + 1 :])
    return jnp.moveaxis(tiles, dim, 0)


def exchange_both(value, axis, axes, splits, concats):
    sizes = [lax.axis_size(a) for a in axes]
    tiles = split_up(value, splits[0], sizes[0])
    tiles = jnp.moveaxis(split_up(tiles, splits[1] + 1, sizes[1]), 0, 1)
    inside = tiles.shape[2:]
    tiles = tiles.reshape(-1, *inside)
    tiles = lax.all_to_all(tiles, axis, split_axis=0, concat_axis=0, tiled=True)
    tiles = joined_along(tiles.reshape(*sizes, *inside), concats[0] + 1)
    return joined_along(tiles, concats[1])


def lookup(values, positions):
    table = jnp.arange(values.shape[0], dtype=jnp.int32)
    matches = positions[:, None] == table[None, :]
    return jnp.sum(jnp.where(matches, values[None, :], 0.0), axis=1)


def shards(amplitudes, df_factors, ladder, occ_energy, occ_index, vir_energy, vir_map):
    rows_tile, cols_tile = amplitudes.shape
    occ_row = rows_tile // VIR
    occ_col = cols_tile // VIR
    occ_all = occ_index.shape[0]
    vir_rows = VIR // lax.axis_size("row")
    vir_cols = VIR // lax.axis_size("col")
    blocks = amplitudes.reshape(occ_row, VIR, occ_col, VIR)
    mirror = jnp.transpose(blocks, (0, 3, 2, 1))
    combined = (2.0 * blocks.astype(jnp.float32) - mirror.astype(jnp.float32)).astype(jnp.bfloat16)
    combined = combined.reshape(rows_tile, cols_tile)
    factors = gather_directly(df_factors, "row", 1)
    partial_fit = jnp.dot(combined, factors, preferred_element_type=jnp.float32)
    contract = (((1,), (1,)), ((), ()))
    shared = lax.psum_scatter(partial_fit, "col", scatter_dimension=1, tiled=True).astype(
        jnp.bfloat16
    )
    fitted = lax.all_gather(shared, "col", axis=1, tiled=True)
    coulomb = lax.dot_general(fitted, factors, contract, preferred_element_type=jnp.float32)
    arranged = exchange_both(blocks, ("row", "col"), ("row", "col"), (1, 3), (0, 2))
    pair_major = jnp.transpose(arranged, (0, 2, 1, 3)).reshape(
        occ_all * occ_all, vir_rows * vir_cols
    )
    hole_wide = jnp.dot(
        lax.all_gather(ladder, ("row", "col"), axis=0, tiled=True),
        pair_major,
        preferred_element_type=jnp.float32,
    )
    hole_term = hole_wide.astype(jnp.bfloat16)
    returned = jnp.transpose(hole_term.reshape(occ_all, occ_all, vir_rows, vir_cols), (0, 2, 1, 3))
    hole_tile = exchange_both(returned, ("row", "col"), ("row", "col"), (0, 2), (1, 3))
    row_start = lax.axis_index("row") * occ_row
    col_start = lax.axis_index("col") * occ_col
    row_energy = lookup(occ_energy, lax.dynamic_slice_in_dim(occ_index, row_start, occ_row))
    col_energy = lookup(occ_energy, lax.dynamic_slice_in_dim(occ_index, col_start, occ_col))
    virtual = lookup(vir_energy, vir_map)
    denominator = (
        row_energy[:, None, None, None]
        + col_energy[None, None, :, None]
        - virtual[None, :, None, None]
        - virtual[None, None, None, :]
    )
    summed = coulomb.reshape(occ_row, VIR, occ_col, VIR) + hole_tile.astype(jnp.float32)
    return (summed / denominator).astype(jnp.bfloat16).reshape(rows_tile, cols_tile)


def solution(mesh):
    placed = (P("row", "col"), P("col", "row"), P(("row", "col"), None), P(), P(), P(), P())
    return jax.shard_map(
        shards, mesh=mesh, in_specs=placed, out_specs=P("row", "col"), check_vma=False
    )
```

profile of v0, /device:TPU:1, one launch (start us, length us, event | category | flops | bytes accessed | tf_op | source)
XLA Modules:
  0.0 958.5 jit_solution(7380441677216063754)
XLA Ops:
  7.4 0.0 copy-start
  7.4 2.0 broadcast_in_dim.26
  9.4 9.6 %all-to-all-start = ((bf16[16,512,64]{1,2,0:T(8,128)(2,1)}), bf16[16,512,64]{1,2,0:T(8,128)(2,1)}, u32[]{:S(2)}, u32[]{:S(2)}) async-start(bf16[16,512,64]{1,2,0:T(8,128)(2,1)} %broadcast_in_dim.26), calls=%async_computation | async-start | bytes 2097152 | tf_op jit(solution)/shard_map/all_to_all | solution.py:17
  19.0 0.0 reduce-scatter.2.cloned.1.call-start
  19.0 0.0 copy-done
  19.0 0.5 copy.97
  19.6 0.3 broadcast_multiply_fusion
  19.9 1.4 fusion
  21.2 22.4 %all-to-all-done = bf16[16,512,64]{1,2,0:T(8,128)(2,1)} async-done(((bf16[16,512,64]{1,2,0:T(8,128)(2,1)}), bf16[16,512,64]{1,2,0:T(8,128)(2,1)}, u32[]{:S(2)}, u32[]{:S(2)}) %all-to-all-start) | async-done | bytes 1048608 | tf_op jit(solution)/shard_map/all_to_all | solution.py:17
  43.7 4.8 fusion.3
  48.4 0.0 reduce-scatter.2.cloned.1.call-update
  48.4 0.0 all-gather.6.cloned.1.call-start
  48.5 0.5 all-gather.6.cloned.1.call-update
  49.0 3.1 copy.100
  52.2 5.0 copy.117
  57.1 7.1 reshape.149
  64.2 20.4 %all-to-all-start.1 = ((bf16[512,2,512]{2,1,0:T(2,128)(2,1)}), bf16[512,2,512]{2,1,0:T(2,128)(2,1)S(1)}, u32[]{:S(2)}, u32[]{:S(2)}) async-start(bf16[512,2,512]{2,1,0:T(2,128)(2,1)} %reshape.149), calls=%async_computation.2 | async-start | bytes 2097152 | tf_op jit(solution)/shard_map/all_to_all | solution.py:38
  84.6 0.2 all-gather.4.cloned.1.call-start
  84.8 74.6 %reduce-scatter.2.cloned.1.call-done = f32[1024,32]{0,1:T(8,128)} async-done(((f32[1024,1024]{0,1:T(8,128)}), f32[1024,32]{0,1:T(8,128)}) %reduce-scatter.2.cloned.1.call-update) | async-done | bytes 131088 | tf_op jit(solution)/shard_map/reduce_scatter | solution.py:63
  159.5 1.5 convert_element_type.55
  161.0 0.0 all-gather.4.cloned.1.call-update
  161.0 0.0 all-to-all-done.1
  161.0 3.6 reshape.150
  164.6 10.4 %copy.118 = bf16[16,32,2,32,1,16]{1,0,5,3,2,4:T(8,128)(2,1)} copy(bf16[16,32,2,32,1,16]{3,5,2,1,0,4:T(8,128)(2,1)} %bitcast.70) | data formatting | bytes 2097152 | tf_op jit(solution)/shard_map/reshape | solution.py:39
  175.0 11.1 %copy.104 = bf16[32,16,2,32,1,16]{3,5,4,2,1,0:T(8,128)(2,1)} copy(bf16[32,16,2,32,1,16]{0,1,5,3,2,4:T(8,128)(2,1)} %bitcast.74) | data formatting | bytes 2097152 | tf_op jit(solution)/shard_map/transpose | solution.py:10
  186.1 11.1 %copy.106 = bf16[32,32,32,16]{1,0,3,2:T(8,128)(2,1)} copy(bf16[32,32,32,16]{2,3,0,1:T(8,128)(2,1)} %bitcast.75) | data formatting | bytes 2097152 | tf_op jit(solution)/shard_map/transpose | solution.py:69
  197.2 6.2 reshape.137
  203.4 627.0 %all-gather.6.cloned.1.call-done = bf16[512,2,1024]{2,1,0:T(2,128)(2,1)} async-done(((bf16[1,2,1024]{2,1,0:T(2,128)(2,1)}), bf16[512,2,1024]{2,1,0:T(2,128)(2,1)}) %all-gather.6.cloned.1.call-update) | async-done | bytes 2097168 | tf_op jit(solution)/shard_map/all_gather | solution.py:73
  830.3 2.7 reshape.147
  833.1 2.3 convolution_convert_fusion
  835.4 1.5 copy.107
  836.8 4.4 reshape.138
  841.2 5.2 copy.123
  846.4 9.4 copy.120
  855.9 7.1 reshape.151
  862.9 0.0 copy-start.4
  862.9 0.0 copy-start.1
  862.9 0.0 copy-start.2
  862.9 0.0 copy-start.3
  863.0 11.9 %all-to-all-start.2 = ((bf16[512,2,512]{2,1,0:T(2,128)(2,1)}), bf16[512,2,512]{2,1,0:T(2,128)(2,1)S(1)}, u32[]{:S(2)}, u32[]{:S(2)}) async-start(bf16[512,2,512]{2,1,0:T(2,128)(2,1)} %reshape.151), calls=%async_computation.3 | async-start | bytes 2097152 | tf_op jit(solution)/shard_map/all_to_all | solution.py:38
  874.9 0.0 copy-done.4
  874.9 0.1 dynamic_slice.6
  875.0 0.7 dynamic_slice.7
  875.6 0.0 copy-done.1
  875.6 1.3 fusion.2
  876.9 0.2 fusion.1
  877.1 0.0 copy-done.2
  877.1 0.0 copy-done.3
  877.1 0.2 select_reduce_fusion
  877.4 0.6 broadcast_add_fusion
  878.0 0.1 broadcast_subtract_fusion
  878.1 30.2 %all-to-all-done.2 = bf16[512,2,512]{2,1,0:T(2,128)(2,1)S(1)} async-done(((bf16[512,2,512]{2,1,0:T(2,128)(2,1)}), bf16[512,2,512]{2,1,0:T(2,128)(2,1)S(1)}, u32[]{:S(2)}, u32[]{:S(2)}) %all-to-all-start.2) | async-done | bytes 1048608 | tf_op jit(solution)/shard_map/all_to_all | solution.py:38
  908.3 3.5 reshape.152
  911.9 5.2 copy.110
  917.1 4.3 reshape.145
  921.5 11.8 %copy.111 = f32[32,2,16,32,1,16]{3,2,5,1,0,4:T(8,128)} copy(f32[32,2,16,32,1,16]{0,2,5,3,1,4:T(8,128)} %bitcast.67) | data formatting | bytes 4194304 | tf_op jit(solution)/shard_map/convert_element_type | solution.py:91
  933.3 6.2 reshape.144
  939.5 1.5 copy.112
  941.0 1.9 copy.113
  943.0 0.0 all-gather.4.cloned.1.call-done
  943.0 3.9 copy.115
  947.0 4.1 divide_convert_fusion
Async XLA Ops:
  7.4 11.7 %copy-start = (bf16[1024,512]{1,0:T(8,128)(2,1)S(1)}, bf16[1024,512]{1,0:T(8,128)(2,1)}, u32[]{:S(2)}) copy-start(bf16[1024,512]{1,0:T(8,128)(2,1)} %param.7) | copy-start | bytes 3145732
  9.4 34.3 %all-to-all-start = ((bf16[16,512,64]{1,2,0:T(8,128)(2,1)}), bf16[16,512,64]{1,2,0:T(8,128)(2,1)}, u32[]{:S(2)}, u32[]{:S(2)}) async-start(bf16[16,512,64]{1,2,0:T(8,128)(2,1)} %broadcast_in_dim.26), calls=%async_computation | async-start | bytes 2097152 | tf_op jit(solution)/shard_map/all_to_all | solution.py:17
  19.0 140.5 %reduce-scatter.2.cloned.1.call-start = ((), (), s32[]{:S(2)}) async-start(), calls=%async_computation.4 | async-start | bytes 4325376 | tf_op jit(solution)/shard_map/reduce_scatter | solution.py:63
  48.4 781.9 %all-gather.6.cloned.1.call-start = ((), (), s32[]{:S(2)}) async-start(), calls=%async_computation.6 | async-start | bytes 2101248 | tf_op jit(solution)/shard_map/all_gather | solution.py:73
  64.2 96.8 %all-to-all-start.1 = ((bf16[512,2,512]{2,1,0:T(2,128)(2,1)}), bf16[512,2,512]{2,1,0:T(2,128)(2,1)S(1)}, u32[]{:S(2)}, u32[]{:S(2)}) async-start(bf16[512,2,512]{2,1,0:T(2,128)(2,1)} %reshape.149), calls=%async_computation.2 | async-start | bytes 2097152 | tf_op jit(solution)/shard_map/all_to_all | solution.py:38
  84.6 858.4 %all-gather.4.cloned.1.call-start = ((), (), s32[]{:S(2)}) async-start(), calls=%async_computation.5 | async-start | bytes 2162688 | tf_op jit(solution)/shard_map/all_gather | solution.py:66
  862.9 11.9 %copy-start.4 = (s32[32]{0:T(128)S(1)}, s32[32]{0:T(128)}, u32[]{:S(2)}) copy-start(s32[32]{0:T(128)} %param.11) | copy-start | bytes 388
  862.9 12.7 %copy-start.1 = (f32[200]{0:T(256)S(1)}, f32[200]{0:T(256)}, u32[]{:S(2)}) copy-start(f32[200]{0:T(256)} %param.10) | copy-start | bytes 2404
  862.9 14.2 %copy-start.2 = (f32[512]{0:T(512)S(1)}, f32[512]{0:T(512)}, u32[]{:S(2)}) copy-start(f32[512]{0:T(512)} %param.12) | copy-start | bytes 6148
  862.9 14.2 %copy-start.3 = (s32[512]{0:T(512)S(1)}, s32[512]{0:T(512)}, u32[]{:S(2)}) copy-start(s32[512]{0:T(512)} %param.13) | copy-start | bytes 6148
  863.0 45.4 %all-to-all-start.2 = ((bf16[512,2,512]{2,1,0:T(2,128)(2,1)}), bf16[512,2,512]{2,1,0:T(2,128)(2,1)S(1)}, u32[]{:S(2)}, u32[]{:S(2)}) async-start(bf16[512,2,512]{2,1,0:T(2,128)(2,1)} %reshape.151), calls=%async_computation.3 | async-start | bytes 2097152 | tf_op jit(solution)/shard_map/all_to_all | solution.py:38
Sparse Core Ops, SparseCore 0:
  48.6 110.8 reduce-scatter.1
Sparse Core Ops, SparseCore 1:
  51.0 779.2 all-gather.5
  833.4 76.3 all-gather.3
where the time goes:
time: 960 us; the launch traced here: 958 us
  waiting for transfers between devices  755 us (79%)
  local copies, waits for them, and re-layouts  130 us (14%)
  starting transfers between devices  42.2 us (4%)
  between operations  15 us (2%)
  matrix products  11.1 us (1%)
    all_gather x1, waiting for transfers between devices, shards(): lax.all_gather(ladder, ('row', 'col'), axis=0, tiled=True)  627 us
    reduce_scatter x1, waiting for transfers between devices, shards(): lax.psum_scatter(partial_fit, 'col', scatter_dimension=1, tiled=True)  74.6 us
    all_to_all x2, starting transfers between devices, exchange_both(): tiles = lax.all_to_all(tiles, axis, split_axis=0, concat_axis=0, tiled=True)  32.3 us
    all_to_all x2, waiting for transfers between devices, exchange_both(): tiles = lax.all_to_all(tiles, axis, split_axis=0, concat_axis=0, tiled=True)  30.2 us
    convert_element_type x5, local copies, waits for them, and re-layouts, shards(): hole_tile.astype(jnp.float32)  25.8 us
    unnamed x15, local copies, waits for them, and re-layouts  24 us
    all_to_all x1, waiting for transfers between devices, from_everyone(): lax.all_to_all(jnp.broadcast_to(value[None], (devices, *value.shape)), ax...  22.4 us
  transfers between devices with their start and end apart: 6, of which 4 were waited for; matrix products, arithmetic and copies ran while one was open for 14% of the time, Pallas kernels for 0%

commit v1 on v0

v1 whole, which is shorter than its diff:
```python
import jax
import jax.numpy as jnp
from jax import lax
from jax.sharding import Mesh, PartitionSpec as P

VIR = 512
BF = jnp.bfloat16
F32 = jnp.float32
CHIPS = ("y", "zl", "zh", "x")


def exchange(value, axes):
    return lax.all_to_all(value, axes, split_axis=0, concat_axis=0, tiled=True)


def spread(value, axes):
    count = lax.axis_size(axes)
    return exchange(jnp.broadcast_to(value[None], (count, *value.shape)), axes)


def partner(value):
    return lax.ppermute(value, "core", [(0, 1), (1, 0)])


def lookup(values, positions):
    table = jnp.arange(values.shape[0], dtype=jnp.int32)
    matches = positions[:, None] == table[None, :]
    return jnp.sum(jnp.where(matches, values[None, :], 0.0), axis=1)


def dot(a, b, ca, cb):
    return lax.dot_general(a, b, (((ca,), (cb,)), ((), ())), preferred_element_type=F32)


def shards(amplitudes, df_factors, ladder, occ_energy, occ_index, vir_energy, vir_map):
    core = lax.axis_index("core")
    blocks = amplitudes.reshape(2, VIR, VIR)
    mirror = jnp.transpose(blocks, (0, 2, 1))
    combined = (2.0 * blocks.astype(F32) - mirror.astype(F32)).astype(BF).reshape(1024, 512)
    combined_other = partner(combined)

    tall = jnp.transpose(df_factors)
    halves = jnp.broadcast_to(tall.reshape(1, 2, 32, 512), (16, 2, 32, 512)).reshape(32, 32, 512)
    factors = exchange(halves, ("y", "zl", "core")).reshape(16, 2, 32, 512)
    own = lax.dynamic_index_in_dim(factors, core, 1, keepdims=False).reshape(512, 512)
    other = lax.dynamic_index_in_dim(factors, 1 - core, 1, keepdims=False).reshape(512, 512)
    partial = (dot(combined, own, 1, 1) + dot(combined_other, other, 1, 1)).astype(BF)
    pieces = exchange(partial.reshape(16, 64, 512), ("zh", "x"))
    shared = jnp.sum(pieces.astype(F32), axis=0).astype(BF)
    fitted = spread(shared, ("zh",))
    fitted = spread(fitted, ("x",))
    fitted = jnp.transpose(fitted, (1, 0, 2, 3)).reshape(1024, 512)
    fitted_other = partner(fitted)
    other_back = partner(other)
    coulomb = dot(fitted, own, 1, 0) + dot(fitted_other, other_back, 1, 0)

    tiles = amplitudes.reshape(2, 64, 8, 4, 128).transpose(1, 3, 0, 2, 4).reshape(256, 2, 8, 128)
    pairs = exchange(tiles, CHIPS).reshape(512, 1024)
    pairs_other = partner(pairs)
    rows = ladder.reshape(2, 16, 2, 16, 2).transpose(0, 4, 1, 3, 2).reshape(2, 2, 512)
    mine = spread(rows, ("y", "zl", "zh")).reshape(64, 2, 2, 512)
    mine = exchange(jnp.broadcast_to(mine.transpose(1, 0, 2, 3)[None], (4, 2, 64, 2, 512)).reshape(8, 64, 2, 512), ("x", "core"))
    mine = mine.reshape(4, 2, 16, 2, 2, 2, 512).transpose(5, 2, 4, 0, 1, 3, 6).reshape(2, 512, 512)
    weight_own = lax.dynamic_index_in_dim(mine, core, 0, keepdims=False)
    weight_other = lax.dynamic_index_in_dim(mine, 1 - core, 0, keepdims=False)
    hole = (dot(weight_own, pairs, 1, 0) + dot(weight_other, pairs_other, 1, 0)).astype(BF)
    hole = exchange(hole.reshape(256, 2, 8, 128), CHIPS)
    hole = hole.reshape(64, 4, 2, 8, 128).transpose(2, 0, 3, 1, 4).reshape(2, VIR, VIR)

    row = lax.axis_index(("y", "zl"))
    col = lax.axis_index(("zh", "x", "core"))
    row_energy = lookup(occ_energy, lax.dynamic_slice_in_dim(occ_index, row * 2, 2))
    col_energy = lookup(occ_energy, lax.dynamic_slice_in_dim(occ_index, col, 1))
    virtual = lookup(vir_energy, vir_map)
    denominator = row_energy[:, None, None] + col_energy[0] - virtual[None, :, None] - virtual[None, None, :]
    summed = coulomb.reshape(2, VIR, VIR) + hole.astype(F32)
    return (summed / denominator).astype(BF).reshape(1024, 512)


def solution(mesh):
    fine = Mesh(mesh.devices.reshape(8, 2, 4, 4, 2), ("y", "zl", "zh", "x", "core"))
    row, col = ("y", "zl"), ("zh", "x", "core")
    placed = (P(row, col), P(col, row), P(row + col, None), P(), P(), P(), P())
    return jax.shard_map(shards, mesh=fine, in_specs=placed, out_specs=P(row, col), check_vma=False)
```

time: 960 us -> 250 us (0.26)
  waiting for transfers between devices: 755 us -> 110 us
  local copies, waits for them, and re-layouts: 130 us -> 28.6 us
  blocking collectives: 0 us -> 30.7 us
  starting transfers between devices: 42.2 us -> 61.5 us
  between operations: 15 us -> 0.29 us
    all_gather x2 -> x0, waiting for transfers between devices: 627 us -> none  [the longest x1 627 us: shards(): lax.all_gather(ladder, ('row', 'col'), axis=0, tiled=True)]
    reduce_scatter x1 -> x0, waiting for transfers between devices: 74.6 us -> none  [shards(): lax.psum_scatter(partial_fit, 'col', scatter_dimension=1, tiled=True)]
    all_to_all x3 -> x7, waiting for transfers between devices: 52.6 us -> 110 us  [exchange(): return lax.all_to_all(value, axes, split_axis=0, concat_axis=0, tiled=True)]
    reshape x5 -> x1, local copies, waits for them, and re-layouts: 35.3 us -> 1.22 us  [shards(): ladder.reshape(2, 16, 2, 16, 2).transpose(0, 4, 1, 3, 2).reshape(2, 2, 512)]
    all_to_all x0 -> x1, blocking collectives: none -> 30.7 us  [exchange(): return lax.all_to_all(value, axes, split_axis=0, concat_axis=0, tiled=True)]
    convert_element_type x7 -> x2, local copies, waits for them, and re-layouts: 27.9 us -> 1.77 us  [the longest x1 1.64 us: shards(): mirror.astype(F32)]
    unnamed x15 -> x20, local copies, waits for them, and re-layouts: 24 us -> 6.31 us
    transpose x3 -> x4, local copies, waits for them, and re-layouts: 25.4 us -> 8.1 us  [the longest x1 3.38 us: shards(): ladder.reshape(2, 16, 2, 16, 2).transpose(0, 4, 1, 3, 2).reshape(2, 2, 512)]
  transfers between devices with their start and end apart: 6 -> 11, of which waited for: 4 -> 8; matrix products, arithmetic and copies ran while one was open for 14% -> 11% of each run, Pallas kernels for 0% -> 0%
where the time goes in v1:
time: 250 us; the launch traced here: 246 us
  waiting for transfers between devices  110 us (44%)
  starting transfers between devices  61.5 us (25%)
  blocking collectives  30.7 us (12%)
  local copies, waits for them, and re-layouts  28.6 us (11%)
  matrix products  11.6 us (5%)
  other arithmetic  3.45 us (1%)
    all_to_all x7, waiting for transfers between devices, exchange(): return lax.all_to_all(value, axes, split_axis=0, concat_axis=0, tiled=True)  110 us
    all_to_all x7, starting transfers between devices, exchange(): return lax.all_to_all(value, axes, split_axis=0, concat_axis=0, tiled=True)  51.1 us
    all_to_all x1, blocking collectives, exchange(): return lax.all_to_all(value, axes, split_axis=0, concat_axis=0, tiled=True)  30.7 us
    dot_general x6, matrix products, dot(): lax.dot_general(a, b, (((ca,), (cb,)), ((), ())), preferred_element_type=...  11.6 us
    ppermute x4, starting transfers between devices, partner(): return lax.ppermute(value, 'core', [(0, 1), (1, 0)])  10.4 us
    unnamed x20, local copies, waits for them, and re-layouts  6.31 us
  transfers between devices with their start and end apart: 11, of which 8 were waited for; matrix products, arithmetic and copies ran while one was open for 11% of the time, Pallas kernels for 0%

profile of v1, /device:TPU:1, one launch (start us, length us, event | category | flops | bytes accessed | tf_op | source)
XLA Modules:
  0.0 246.1 jit_solution(11530986620591732555)
XLA Ops:
  0.0 1.2 reshape.121
  1.2 3.4 %copy.34 = bf16[2,2,16,16,2]{4,3,2,1,0:T(8,128)(2,1)S(1)} copy(bf16[2,2,16,16,2]{1,3,4,2,0:T(8,128)(2,1)S(1)} %bitcast.86) | data formatting | bytes 8192 | tf_op jit(solution)/shard_map/transpose | solution.py:60
  4.6 0.0 copy-start
  4.6 0.3 broadcast_in_dim.46
  4.9 0.1 broadcast_in_dim.47
  5.1 30.7 %all_to_all.40 = bf16[64,2,2,512]{3,2,1,0:T(2,128)(2,1)} all-to-all(bf16[64,2,2,512]{3,2,1,0:T(2,128)(2,1)S(1)} %broadcast_in_dim.47), channel_id=1, replica_groups=mesh['y'=8,'zl'=2,'zh'=4,'x'=4,'core'=2] {'y','zl','zh'}, dimensions={0} | all-to-all | bytes 524288 | tf_op jit(solution)/shard_map/all_to_all | solution.py:13
  35.8 1.9 broadcast_in_dim.39
  37.7 6.5 %all-to-all-start = ((bf16[32,32,512]{2,1,0:T(8,128)(2,1)}), bf16[32,32,512]{2,1,0:T(8,128)(2,1)S(1)}, u32[]{:S(2)}, u32[]{:S(2)}) async-start(bf16[32,32,512]{2,1,0:T(8,128)(2,1)} %bitcast.6), calls=%async_computation | async-start | bytes 2097152 | tf_op jit(solution)/shard_map/all_to_all | solution.py:13
  44.2 0.0 copy-done
  44.2 1.3 copy.37
  45.5 26.7 %all-to-all-done = bf16[32,32,512]{2,1,0:T(8,128)(2,1)S(1)} async-done(((bf16[32,32,512]{2,1,0:T(8,128)(2,1)}), bf16[32,32,512]{2,1,0:T(8,128)(2,1)S(1)}, u32[]{:S(2)}, u32[]{:S(2)}) %all-to-all-start) | async-done | bytes 1048608 | tf_op jit(solution)/shard_map/all_to_all | solution.py:13
  72.2 1.0 copy-done.2
  73.2 10.8 %all-to-all-start.6 = ((bf16[256,2,8,128]{3,2,1,0:T(8,128)(2,1)}), bf16[256,2,8,128]{3,2,1,0:T(8,128)(2,1)S(1)}, u32[]{:S(2)}, u32[]{:S(2)}) async-start(bf16[256,2,8,128]{3,2,1,0:T(8,128)(2,1)} %bitcast.79), calls=%async_computation.6 | async-start | bytes 2097152 | tf_op jit(solution)/shard_map/all_to_all | solution.py:13
  84.0 1.6 copy.32
  85.6 0.3 broadcast_multiply_fusion
  85.9 1.3 copy-done.1
  87.2 0.6 fusion
  87.8 2.7 %collective-permute-start = (bf16[1024,512]{1,0:T(8,128)(2,1)S(1)}, bf16[1024,512]{1,0:T(8,128)(2,1)}, u32[]{:S(2)}, u32[]{:S(2)}) collective-permute-start(bf16[1024,512]{1,0:T(8,128)(2,1)S(1)} %bitcast.75), channel_id=1, source_target_pairs={{0,1},{1,0},{2,3},{3,2},{4,5},{5,4},{6,7},{7,6},{8,9},{9,8},{10,11... | collective-permute-start | bytes 3145736 | tf_op jit(solution)/shard_map/ppermute | solution.py:22
  90.5 1.3 constant_dynamic-slice_fusion.2
  91.8 0.7 fusion.9
  92.6 0.3 collective-permute-done
  92.9 3.0 %add_convert_fusion.1 = bf16[1024,512]{1,0:T(8,128)(2,1)} fusion(f32[1024,512]{1,0:T(8,128)S(1)} %fusion.9, bf16[1024,512]{1,0:T(8,128)(2,1)} %collective-permute-done, bf16[512,512]{1,0:T(8,128)(2,1)S(1)} %bitcast.83), kind=kOutput, calls=%fused_computation.4 | convolution fusion | flops 537919488 | bytes 4718592 | tf_op jit(solution)/shard_map/dot_general | solution.py:32
  95.9 17.9 %all-to-all-done.6 = bf16[256,2,8,128]{3,2,1,0:T(8,128)(2,1)S(1)} async-done(((bf16[256,2,8,128]{3,2,1,0:T(8,128)(2,1)}), bf16[256,2,8,128]{3,2,1,0:T(8,128)(2,1)S(1)}, u32[]{:S(2)}, u32[]{:S(2)}) %all-to-all-start.6) | async-done | bytes 1048608 | tf_op jit(solution)/shard_map/all_to_all | solution.py:13
  113.8 3.7 %all-to-all-start.1 = ((bf16[16,64,512]{2,1,0:T(8,128)(2,1)}), bf16[16,64,512]{2,1,0:T(8,128)(2,1)S(1)}, u32[]{:S(2)}, u32[]{:S(2)}) async-start(bf16[16,64,512]{2,1,0:T(8,128)(2,1)} %bitcast.81), calls=%async_computation.1 | async-start | bytes 2097152 | tf_op jit(solution)/shard_map/all_to_all | solution.py:13
  117.4 1.1 copy.35
  118.6 25.9 %all-to-all-done.1 = bf16[16,64,512]{2,1,0:T(8,128)(2,1)S(1)} async-done(((bf16[16,64,512]{2,1,0:T(8,128)(2,1)}), bf16[16,64,512]{2,1,0:T(8,128)(2,1)S(1)}, u32[]{:S(2)}, u32[]{:S(2)}) %all-to-all-start.1) | async-done | bytes 1048608 | tf_op jit(solution)/shard_map/all_to_all | solution.py:13
  144.5 1.5 broadcast_in_dim.78
  146.0 7.3 %all-to-all-start.5 = ((bf16[8,64,2,512]{3,2,1,0:T(2,128)(2,1)}), bf16[8,64,2,512]{3,2,1,0:T(2,128)(2,1)}, u32[]{:S(2)}, u32[]{:S(2)}) async-start(bf16[8,64,2,512]{3,2,1,0:T(2,128)(2,1)} %bitcast.16), calls=%async_computation.5 | async-start | bytes 2097152 | tf_op jit(solution)/shard_map/all_to_all | solution.py:13
  153.4 1.3 copy.54
  154.6 2.0 collective-permute-start.3
  156.7 0.2 reduce_sum.39
  156.8 11.6 %all-to-all-done.5 = bf16[8,64,2,512]{3,2,1,0:T(2,128)(2,1)} async-done(((bf16[8,64,2,512]{3,2,1,0:T(2,128)(2,1)}), bf16[8,64,2,512]{3,2,1,0:T(2,128)(2,1)}, u32[]{:S(2)}, u32[]{:S(2)}) %all-to-all-start.5) | async-done | bytes 1048608 | tf_op jit(solution)/shard_map/all_to_all | solution.py:13
  168.5 0.7 broadcast_in_dim.40
  169.2 3.6 %all-to-all-start.2 = ((bf16[4,64,512]{2,1,0:T(8,128)(2,1)}), bf16[4,64,512]{2,1,0:T(8,128)(2,1)S(1)}, u32[]{:S(2)}, u32[]{:S(2)}) async-start(bf16[4,64,512]{2,1,0:T(8,128)(2,1)} %broadcast_in_dim.40), calls=%async_computation.2 | async-start | bytes 524288 | tf_op jit(solution)/shard_map/all_to_all | solution.py:13
  172.8 2.3 copy.36
  175.1 5.7 %all-to-all-done.2 = bf16[4,64,512]{2,1,0:T(8,128)(2,1)S(1)} async-done(((bf16[4,64,512]{2,1,0:T(8,128)(2,1)}), bf16[4,64,512]{2,1,0:T(8,128)(2,1)S(1)}, u32[]{:S(2)}, u32[]{:S(2)}) %all-to-all-start.2) | async-done | bytes 262176 | tf_op jit(solution)/shard_map/all_to_all | solution.py:13
  180.8 1.1 broadcast_in_dim.45
  181.9 4.2 %all-to-all-start.3 = ((bf16[4,4,64,512]{3,2,1,0:T(8,128)(2,1)}), bf16[4,4,64,512]{3,2,1,0:T(8,128)(2,1)}, u32[]{:S(2)}, u32[]{:S(2)}) async-start(bf16[4,4,64,512]{3,2,1,0:T(8,128)(2,1)} %broadcast_in_dim.45), calls=%async_computation.3 | async-start | bytes 2097152 | tf_op jit(solution)/shard_map/all_to_all | solution.py:13
  186.2 2.2 constant_dynamic-slice_fusion
  188.4 0.7 fusion.4
  189.1 0.0 collective-permute-done.3
  189.1 2.0 fusion.1
  191.0 0.0 copy-start.7
  191.0 1.2 copy.42
  192.3 5.7 %all-to-all-done.3 = bf16[4,4,64,512]{3,2,1,0:T(8,128)(2,1)} async-done(((bf16[4,4,64,512]{3,2,1,0:T(8,128)(2,1)}), bf16[4,4,64,512]{3,2,1,0:T(8,128)(2,1)}, u32[]{:S(2)}, u32[]{:S(2)}) %all-to-all-start.3) | async-done | bytes 1048608 | tf_op jit(solution)/shard_map/all_to_all | solution.py:13
  198.0 15.0 %all-to-all-start.7 = ((bf16[256,2,8,128]{3,2,1,0:T(8,128)(2,1)}), bf16[256,2,8,128]{3,2,1,0:T(8,128)(2,1)S(1)}, u32[]{:S(2)}, u32[]{:S(2)}) async-start(bf16[256,2,8,128]{3,2,1,0:T(8,128)(2,1)} %bitcast.41), calls=%async_computation.7 | async-start | bytes 2097152 | tf_op jit(solution)/shard_map/all_to_all | solution.py:13
  213.0 0.0 copy-done.7
  213.0 0.6 dynamic_slice.25
  213.6 1.3 copy.33
  214.9 3.8 %collective-permute-start.1 = (bf16[1024,512]{1,0:T(8,128)(2,1)S(1)}, bf16[1024,512]{1,0:T(8,128)(2,1)}, u32[]{:S(2)}, u32[]{:S(2)}) collective-permute-start(bf16[1024,512]{1,0:T(8,128)(2,1)S(1)} %bitcast.77), channel_id=1, source_target_pairs={{0,1},{1,0},{2,3},{3,2},{4,5},{5,4},{6,7},{7,6},{8,9},{9,8},{10,11... | collective-permute-start | bytes 3145736 | tf_op jit(solution)/shard_map/ppermute | solution.py:22
  218.7 1.3 fusion.8
  220.0 0.1 dynamic_slice.24
  220.1 0.2 fusion.7
  220.3 0.7 broadcast_add_fusion
  221.0 1.9 collective-permute-start.2
  222.9 0.1 broadcast_bitcast_fusion
  223.0 0.2 select_reduce_fusion
  223.3 2.0 fusion.10
  225.3 16.0 %all-to-all-done.7 = bf16[256,2,8,128]{3,2,1,0:T(8,128)(2,1)S(1)} async-done(((bf16[256,2,8,128]{3,2,1,0:T(8,128)(2,1)}), bf16[256,2,8,128]{3,2,1,0:T(8,128)(2,1)S(1)}, u32[]{:S(2)}, u32[]{:S(2)}) %all-to-all-start.7) | async-done | bytes 1048608 | tf_op jit(solution)/shard_map/all_to_all | solution.py:13
  241.3 0.1 copy.38
  241.5 0.0 collective-permute-done.2
  241.5 0.0 collective-permute-done.1
  241.5 1.4 copy-done.3
  242.9 3.2 %divide_convert_fusion = bf16[1024,512]{1,0:T(8,128)(2,1)} fusion(f32[1024,512]{1,0:T(8,128)S(1)} %bitcast.82, f32[1024,512]{1,0:T(8,128)S(1)} %copy-done.3, bf16[1024,512]{1,0:T(8,128)(2,1)} %collective-permute-done.1, bf16[512,512]{1,0:T(8,128)(2,1)} %collective-permute-done.2, f32[512]{0:T(512)S(1)} %select_reduce_fusion, f32[1024]{0:T(1024)S(1)} %sub.49), kind=kOutput, calls=%fused_computation.2 | convolution fusion | flops 539492352 | bytes 6821888 | tf_op jit(solution)/shard_map/dot_general | solution.py:32
  (12 shorter events, 0.0 us)
Async XLA Ops:
  4.6 39.6 %copy-start = (bf16[1024,512]{1,0:T(8,128)(2,1)S(1)}, bf16[1024,512]{1,0:T(8,128)(2,1)}, u32[]{:S(2)}) copy-start(bf16[1024,512]{1,0:T(8,128)(2,1)} %param.7) | copy-start | bytes 3145732
  37.7 34.5 %all-to-all-start = ((bf16[32,32,512]{2,1,0:T(8,128)(2,1)}), bf16[32,32,512]{2,1,0:T(8,128)(2,1)S(1)}, u32[]{:S(2)}, u32[]{:S(2)}) async-start(bf16[32,32,512]{2,1,0:T(8,128)(2,1)} %bitcast.6), calls=%async_computation | async-start | bytes 2097152 | tf_op jit(solution)/shard_map/all_to_all | solution.py:13
  72.2 1.0 copy-start.2
  73.2 40.6 %all-to-all-start.6 = ((bf16[256,2,8,128]{3,2,1,0:T(8,128)(2,1)}), bf16[256,2,8,128]{3,2,1,0:T(8,128)(2,1)S(1)}, u32[]{:S(2)}, u32[]{:S(2)}) async-start(bf16[256,2,8,128]{3,2,1,0:T(8,128)(2,1)} %bitcast.79), calls=%async_computation.6 | async-start | bytes 2097152 | tf_op jit(solution)/shard_map/all_to_all | solution.py:13
  85.6 1.6 copy-start.1
  87.8 5.1 %collective-permute-start = (bf16[1024,512]{1,0:T(8,128)(2,1)S(1)}, bf16[1024,512]{1,0:T(8,128)(2,1)}, u32[]{:S(2)}, u32[]{:S(2)}) collective-permute-start(bf16[1024,512]{1,0:T(8,128)(2,1)S(1)} %bitcast.75), channel_id=1, source_target_pairs={{0,1},{1,0},{2,3},{3,2},{4,5},{5,4},{6,7},{7,6},{8,9},{9,8},{10,11... | collective-permute-start | bytes 3145736 | tf_op jit(solution)/shard_map/ppermute | solution.py:22
  113.8 30.7 %all-to-all-start.1 = ((bf16[16,64,512]{2,1,0:T(8,128)(2,1)}), bf16[16,64,512]{2,1,0:T(8,128)(2,1)S(1)}, u32[]{:S(2)}, u32[]{:S(2)}) async-start(bf16[16,64,512]{2,1,0:T(8,128)(2,1)} %bitcast.81), calls=%async_computation.1 | async-start | bytes 2097152 | tf_op jit(solution)/shard_map/all_to_all | solution.py:13
  146.0 22.4 %all-to-all-start.5 = ((bf16[8,64,2,512]{3,2,1,0:T(2,128)(2,1)}), bf16[8,64,2,512]{3,2,1,0:T(2,128)(2,1)}, u32[]{:S(2)}, u32[]{:S(2)}) async-start(bf16[8,64,2,512]{3,2,1,0:T(2,128)(2,1)} %bitcast.16), calls=%async_computation.5 | async-start | bytes 2097152 | tf_op jit(solution)/shard_map/all_to_all | solution.py:13
  154.6 34.4 %collective-permute-start.3 = (bf16[512,1024]{1,0:T(8,128)(2,1)}, bf16[512,1024]{1,0:T(8,128)(2,1)}, u32[]{:S(2)}, u32[]{:S(2)}) collective-permute-start(bf16[512,1024]{1,0:T(8,128)(2,1)} %bitcast.66), channel_id=1, source_target_pairs={{0,1},{1,0},{2,3},{3,2},{4,5},{5,4},{6,7},{7,6},{8,9},{9,8},{10,11... | collective-permute-start | bytes 3145736 | tf_op jit(solution)/shard_map/ppermute | solution.py:22
  169.2 11.6 %all-to-all-start.2 = ((bf16[4,64,512]{2,1,0:T(8,128)(2,1)}), bf16[4,64,512]{2,1,0:T(8,128)(2,1)S(1)}, u32[]{:S(2)}, u32[]{:S(2)}) async-start(bf16[4,64,512]{2,1,0:T(8,128)(2,1)} %broadcast_in_dim.40), calls=%async_computation.2 | async-start | bytes 524288 | tf_op jit(solution)/shard_map/all_to_all | solution.py:13
  181.9 16.0 %all-to-all-start.3 = ((bf16[4,4,64,512]{3,2,1,0:T(8,128)(2,1)}), bf16[4,4,64,512]{3,2,1,0:T(8,128)(2,1)}, u32[]{:S(2)}, u32[]{:S(2)}) async-start(bf16[4,4,64,512]{3,2,1,0:T(8,128)(2,1)} %broadcast_in_dim.45), calls=%async_computation.3 | async-start | bytes 2097152 | tf_op jit(solution)/shard_map/all_to_all | solution.py:13
  191.0 22.0 %copy-start.7 = (s32[32]{0:T(128)S(1)}, s32[32]{0:T(128)}, u32[]{:S(2)}) copy-start(s32[32]{0:T(128)} %param.11) | copy-start | bytes 388
  198.0 20.8 %copy-start.4 = (f32[200]{0:T(256)S(1)}, f32[200]{0:T(256)}, u32[]{:S(2)}) copy-start(f32[200]{0:T(256)} %param.10) | copy-start | bytes 2404
  198.0 25.0 %copy-start.5 = (f32[512]{0:T(512)S(1)}, f32[512]{0:T(512)}, u32[]{:S(2)}) copy-start(f32[512]{0:T(512)} %param.12) | copy-start | bytes 6148
  198.0 25.0 %copy-start.6 = (s32[512]{0:T(512)S(1)}, s32[512]{0:T(512)}, u32[]{:S(2)}) copy-start(s32[512]{0:T(512)} %param.13) | copy-start | bytes 6148
  198.0 43.3 %all-to-all-start.7 = ((bf16[256,2,8,128]{3,2,1,0:T(8,128)(2,1)}), bf16[256,2,8,128]{3,2,1,0:T(8,128)(2,1)S(1)}, u32[]{:S(2)}, u32[]{:S(2)}) async-start(bf16[256,2,8,128]{3,2,1,0:T(8,128)(2,1)} %bitcast.41), calls=%async_computation.7 | async-start | bytes 2097152 | tf_op jit(solution)/shard_map/all_to_all | solution.py:13
  214.9 26.5 %collective-permute-start.1 = (bf16[1024,512]{1,0:T(8,128)(2,1)S(1)}, bf16[1024,512]{1,0:T(8,128)(2,1)}, u32[]{:S(2)}, u32[]{:S(2)}) collective-permute-start(bf16[1024,512]{1,0:T(8,128)(2,1)S(1)} %bitcast.77), channel_id=1, source_target_pairs={{0,1},{1,0},{2,3},{3,2},{4,5},{5,4},{6,7},{7,6},{8,9},{9,8},{10,11... | collective-permute-start | bytes 3145736 | tf_op jit(solution)/shard_map/ppermute | solution.py:22
  221.0 20.5 %collective-permute-start.2 = (bf16[512,512]{1,0:T(8,128)(2,1)S(1)}, bf16[512,512]{1,0:T(8,128)(2,1)}, u32[]{:S(2)}, u32[]{:S(2)}) collective-permute-start(bf16[512,512]{1,0:T(8,128)(2,1)S(1)} %bitcast.84), channel_id=1, source_target_pairs={{0,1},{1,0},{2,3},{3,2},{4,5},{5,4},{6,7},{7,6},{8,9},{9,8},{10,11... | collective-permute-start | bytes 1572872 | tf_op jit(solution)/shard_map/ppermute | solution.py:22
  241.3 1.6 copy-start.3

commit v2 on v1

v2 whole, which is shorter than its diff:
```python
import jax
import jax.numpy as jnp
from jax import lax
from jax.sharding import Mesh, PartitionSpec as P

VIR = 512
BF = jnp.bfloat16
F32 = jnp.float32
CHIPS = ("y", "zl", "zh", "x")


def exchange(value, axes):
    return lax.all_to_all(value, axes, split_axis=0, concat_axis=0, tiled=True)


def shifted(value, axis, step):
    count = lax.axis_size(axis)
    return lax.ppermute(value, axis, [(i, (i + step) % count) for i in range(count)])


def partner(value):
    return shifted(value, "core", 1)


def gather_ring(value, axis):
    count = lax.axis_size(axis)
    me = lax.axis_index(axis)
    everyone = jnp.zeros((count, *value.shape), value.dtype)
    for step in range(count):
        near = shifted(value, axis, step) if step else value
        everyone = lax.dynamic_update_index_in_dim(everyone, near, (me - step) % count, 0)
    return everyone


def pieces_ring(value, axis):
    count = lax.axis_size(axis)
    me = lax.axis_index(axis)
    pieces = []
    for step in range(count):
        piece = lax.dynamic_index_in_dim(value, (me + step) % count, 0, keepdims=False)
        pieces.append(shifted(piece, axis, step) if step else piece)
    return pieces


def spread(value, axes):
    count = lax.axis_size(axes)
    return exchange(jnp.broadcast_to(value[None], (count, *value.shape)), axes)


def lookup(values, positions):
    table = jnp.arange(values.shape[0], dtype=jnp.int32)
    matches = positions[:, None] == table[None, :]
    return jnp.sum(jnp.where(matches, values[None, :], 0.0), axis=1)


def dot(a, b, ca, cb):
    return lax.dot_general(a, b, (((ca,), (cb,)), ((), ())), preferred_element_type=F32)


def shards(amplitudes, df_factors, ladder, occ_energy, occ_index, vir_energy, vir_map):
    core = lax.axis_index("core")
    blocks = amplitudes.reshape(2, VIR, VIR)

    tall = jnp.transpose(df_factors).reshape(2, 4, 8, 4, 128).transpose(0, 1, 3, 2, 4).reshape(2, 16, 8, 128)
    place = jnp.arange(1024, dtype=jnp.int32)
    source = (place // 32 % 16) * 64 + (place % 2) * 32 + (place // 2 % 16) * 2 + place // 512
    chosen = (jnp.arange(1024, dtype=jnp.int32)[:, None] == source[None, :]).astype(BF)
    rows = dot(ladder, chosen, 1, 0).astype(BF)
    swapped = jnp.concatenate([rows[1:, 512:], rows[1:, :512]], axis=1)
    rows = jnp.concatenate([rows[:1], swapped]).reshape(2, 1, 8, 128)
    send = jnp.concatenate([tall, rows], axis=1)
    send = jnp.broadcast_to(send[None], (16, 2, 17, 8, 128)).reshape(32, 17, 8, 128)
    arrived = exchange(send, ("y", "zl", "core"))
    factors = arrived[:, :16].reshape(16, 2, 4, 4, 8, 128).transpose(0, 1, 2, 4, 3, 5).reshape(16, 2, 32, 512)
    own = lax.dynamic_index_in_dim(factors, core, 1, keepdims=False).reshape(512, 512)
    other = lax.dynamic_index_in_dim(factors, 1 - core, 1, keepdims=False).reshape(512, 512)

    tiles = amplitudes.reshape(2, 64, 8, 4, 128).transpose(1, 3, 0, 2, 4).reshape(256, 2, 8, 128)
    pairs = exchange(tiles, CHIPS)
    weights = gather_ring(arrived[:, 16].reshape(32, 1024), "zh")
    weights = gather_ring(weights, "x")
    weights = weights.reshape(512, 1024)

    mirror = jnp.transpose(blocks, (0, 2, 1))
    combined = (2.0 * blocks.astype(F32) - mirror.astype(F32)).astype(BF).reshape(1024, 512)
    combined_other = partner(combined)
    partial = (dot(combined, own, 1, 1) + dot(combined_other, other, 1, 1)).astype(BF)
    pieces = pieces_ring(partial.reshape(4, 256, 512), "x")
    shared = sum(piece.astype(F32) for piece in pieces)
    shared = exchange(shared.reshape(4, 64, 512), ("zh",))
    shared = jnp.sum(shared, axis=0).astype(BF)
    fitted = spread(shared, ("zh",)).reshape(256, 512)
    fitted = gather_ring(fitted, "x").reshape(1024, 512)
    fitted_other = partner(fitted)
    other_back = partner(other)
    coulomb = dot(fitted, own, 1, 0) + dot(fitted_other, other_back, 1, 0)

    pairs = pairs.reshape(512, 1024)
    pairs_other = partner(pairs)
    hole = (dot(weights[:, :512], pairs, 1, 0) + dot(weights[:, 512:], pairs_other, 1, 0)).astype(BF)
    hole = hole.reshape(4, 2, 2, 16, 2, 8, 128).transpose(3, 2, 0, 4, 1, 5, 6).reshape(256, 2, 8, 128)
    hole = exchange(hole, CHIPS)
    hole = hole.reshape(64, 4, 2, 8, 128).transpose(2, 0, 3, 1, 4).reshape(2, VIR, VIR)

    row = lax.axis_index(("y", "zl"))
    col = lax.axis_index(("zh", "x", "core"))
    row_energy = lookup(occ_energy, lax.dynamic_slice_in_dim(occ_index, row * 2, 2))
    col_energy = lookup(occ_energy, lax.dynamic_slice_in_dim(occ_index, col, 1))
    virtual = lookup(vir_energy, vir_map)
    denominator = row_energy[:, None, None] + col_energy[0] - virtual[None, :, None] - virtual[None, None, :]
    summed = coulomb.reshape(2, VIR, VIR) + hole.astype(F32)
    return (summed / denominator).astype(BF).reshape(1024, 512)


def solution(mesh):
    fine = Mesh(mesh.devices.reshape(8, 2, 4, 4, 2), ("y", "zl", "zh", "x", "core"))
    row, col = ("y", "zl"), ("zh", "x", "core")
    placed = (P(row, col), P(col, row), P(row + col, None), P(), P(), P(), P())

    return jax.shard_map(shards, mesh=fine, in_specs=placed, out_specs=P(row, col), check_vma=False)
```

time: 250 us -> 217 us (0.87)
  starting transfers between devices: 61.5 us -> 103 us
  blocking collectives: 30.7 us -> 0 us
  waiting for transfers between devices: 110 us -> 80.6 us
  local copies, waits for them, and re-layouts: 28.6 us -> 16 us
    all_to_all x7 -> x5, waiting for transfers between devices: 110 us -> 52.4 us  [exchange(): return lax.all_to_all(value, axes, split_axis=0, concat_axis=0, tiled=True)]
    ppermute x4 -> x16, starting transfers between devices: 10.4 us -> 48.7 us  [shifted(): lax.ppermute(value, axis, [(i, (i + step) % count) for i in range(count)])]
    all_to_all x1 -> x0, blocking collectives: 30.7 us -> none  [exchange(): return lax.all_to_all(value, axes, split_axis=0, concat_axis=0, tiled=True)]
    ppermute x4 -> x16, waiting for transfers between devices: 0.35 us -> 28.1 us  [shifted(): lax.ppermute(value, axis, [(i, (i + step) % count) for i in range(count)])]
    transpose x3 -> x0, local copies, waits for them, and re-layouts: 6.82 us -> none  [the longest x1 3.38 us: shards(): ladder.reshape(2, 16, 2, 16, 2).transpose(0, 4, 1, 3, 2).reshape(2, 2, 512)]
    all_to_all x7 -> x5, starting transfers between devices: 51.1 us -> 54 us  [exchange(): return lax.all_to_all(value, axes, split_axis=0, concat_axis=0, tiled=True)]
    unnamed x20 -> x36, local copies, waits for them, and re-layouts: 6.31 us -> 5.08 us
    dot_general x6 -> x7, matrix products: 11.6 us -> 11.1 us  [dot(): lax.dot_general(a, b, (((ca,), (cb,)), ((), ())), preferred_element_type=...]
  transfers between devices with their start and end apart: 11 -> 21, of which waited for: 8 -> 9; matrix products, arithmetic and copies ran while one was open for 11% -> 10% of each run, Pallas kernels for 0% -> 0%
where the time goes in v2:
time: 217 us; the launch traced here: 216 us
  starting transfers between devices  103 us (47%)
  waiting for transfers between devices  80.6 us (37%)
  local copies, waits for them, and re-layouts  16 us (7%)
  matrix products  11.1 us (5%)
  other arithmetic  4.35 us (2%)
    all_to_all x5, starting transfers between devices, exchange(): return lax.all_to_all(value, axes, split_axis=0, concat_axis=0, tiled=True)  54 us
    all_to_all x5, waiting for transfers between devices, exchange(): return lax.all_to_all(value, axes, split_axis=0, concat_axis=0, tiled=True)  52.4 us
    ppermute x16, starting transfers between devices, shifted(): lax.ppermute(value, axis, [(i, (i + step) % count) for i in range(count)])  48.7 us
    ppermute x16, waiting for transfers between devices, shifted(): lax.ppermute(value, axis, [(i, (i + step) % count) for i in range(count)])  28.1 us
    dot_general x7, matrix products, dot(): lax.dot_general(a, b, (((ca,), (cb,)), ((), ())), preferred_element_type=...  11.1 us
    unnamed x36, local copies, waits for them, and re-layouts  5.08 us
  transfers between devices with their start and end apart: 21, of which 9 were waited for; matrix products, arithmetic and copies ran while one was open for 10% of the time, Pallas kernels for 0%

profile of v2, /device:TPU:1, one launch (start us, length us, event | category | flops | bytes accessed | tf_op | source)
XLA Modules:
  0.0 215.5 jit_solution(15363823446100073103)
XLA Ops:
  0.0 2.5 %copy.26 = bf16[64,4,2,8,128]{4,3,2,1,0:T(8,128)(2,1)} copy(bf16[64,4,2,8,128]{4,3,1,0,2:T(8,128)(2,1)} %bitcast.117) | data formatting | bytes 2097152 | tf_op jit(solution)/shard_map/transpose | solution.py:78
  2.5 23.3 %all-to-all-start.3 = ((bf16[256,2,8,128]{3,2,1,0:T(8,128)(2,1)}), bf16[256,2,8,128]{3,2,1,0:T(8,128)(2,1)S(1)}, u32[]{:S(2)}, u32[]{:S(2)}) async-start(bf16[256,2,8,128]{3,2,1,0:T(8,128)(2,1)} %bitcast.40), calls=%async_computation.3 | async-start | bytes 2097152 | tf_op jit(solution)/shard_map/all_to_all | solution.py:13
  25.9 0.7 fusion.5
  26.7 28.7 %all-to-all-done.3 = bf16[256,2,8,128]{3,2,1,0:T(8,128)(2,1)S(1)} async-done(((bf16[256,2,8,128]{3,2,1,0:T(8,128)(2,1)}), bf16[256,2,8,128]{3,2,1,0:T(8,128)(2,1)S(1)}, u32[]{:S(2)}, u32[]{:S(2)}) %all-to-all-start.3) | async-done | bytes 1048608 | tf_op jit(solution)/shard_map/all_to_all | solution.py:13
  55.4 1.2 broadcast_in_dim.103
  56.6 6.2 %all-to-all-start = ((bf16[32,17,8,128]{3,2,1,0:T(8,128)(2,1)}), bf16[32,17,8,128]{3,2,1,0:T(8,128)(2,1)S(1)}, u32[]{:S(2)}, u32[]{:S(2)}) async-start(bf16[32,17,8,128]{3,2,1,0:T(8,128)(2,1)} %bitcast.122), calls=%async_computation | async-start | bytes 2228224 | tf_op jit(solution)/shard_map/all_to_all | solution.py:13
  62.8 1.7 copy.24
  64.5 0.3 broadcast_multiply_fusion
  64.8 1.3 copy-done.2
  66.1 0.6 fusion.1
  66.7 2.3 %collective-permute-start = (bf16[1024,512]{1,0:T(8,128)(2,1)S(1)}, bf16[1024,512]{1,0:T(8,128)(2,1)}, u32[]{:S(2)}, u32[]{:S(2)}) collective-permute-start(bf16[1024,512]{1,0:T(8,128)(2,1)S(1)} %bitcast.123), channel_id=1, source_target_pairs={{0,1},{1,0},{2,3},{3,2},{4,5},{5,4},{6,7},{7,6},{8,9},{9,8},{10,11... | collective-permute-start | bytes 3145736 | tf_op jit(solution)/shard_map/ppermute | solution.py:18
  69.1 1.3 copy.38
  70.3 2.1 collective-permute-start.15
  72.4 19.8 %all-to-all-done = bf16[32,17,8,128]{3,2,1,0:T(8,128)(2,1)S(1)} async-done(((bf16[32,17,8,128]{3,2,1,0:T(8,128)(2,1)}), bf16[32,17,8,128]{3,2,1,0:T(8,128)(2,1)S(1)}, u32[]{:S(2)}, u32[]{:S(2)}) %all-to-all-start) | async-done | bytes 1114144 | tf_op jit(solution)/shard_map/all_to_all | solution.py:13
  92.3 3.4 %collective-permute-start.9 = (bf16[32,1024]{1,0:T(8,128)(2,1)S(1)}, bf16[32,1024]{1,0:T(8,128)(2,1)S(1)}, u32[]{:S(2)}, u32[]{:S(2)}) collective-permute-start(bf16[32,1024]{1,0:T(8,128)(2,1)S(1)} %bitcast.145), channel_id=1, source_target_pairs={{0,8},{8,16},{16,24},{24,0},{1,9},{9,17},{17,25},{25,1},{2,10},{10... | collective-permute-start | bytes 196616 | tf_op jit(solution)/shard_map/ppermute | solution.py:18
  95.7 4.2 %collective-permute-start.10 = (bf16[32,1024]{1,0:T(8,128)(2,1)S(1)}, bf16[32,1024]{1,0:T(8,128)(2,1)S(1)}, u32[]{:S(2)}, u32[]{:S(2)}) collective-permute-start(bf16[32,1024]{1,0:T(8,128)(2,1)S(1)} %bitcast.146), channel_id=1, source_target_pairs={{0,16},{8,24},{16,0},{24,8},{1,17},{9,25},{17,1},{25,9},{2,18},{10... | collective-permute-start | bytes 196616 | tf_op jit(solution)/shard_map/ppermute | solution.py:18
  100.0 0.1 slice.31
  100.1 0.1 constant_dynamic-slice_fusion
  100.2 0.7 fusion.33
  101.0 2.0 add_convert_fusion.1
  103.0 2.2 %collective-permute-start.1 = (bf16[256,512]{1,0:T(8,128)(2,1)S(1)}, bf16[256,512]{1,0:T(8,128)(2,1)S(1)}, u32[]{:S(2)}, u32[]{:S(2)}) collective-permute-start(bf16[256,512]{1,0:T(8,128)(2,1)S(1)} %get-tuple-element.5), channel_id=1, source_target_pairs={{0,2},{2,4},{4,6},{6,0},{1,3},{3,5},{5,7},{7,1},{8,10},{10,12},{12... | collective-permute-start | bytes 786440 | tf_op jit(solution)/shard_map/ppermute | solution.py:18
  105.2 3.6 %collective-permute-start.2 = (bf16[256,512]{1,0:T(8,128)(2,1)S(1)}, bf16[256,512]{1,0:T(8,128)(2,1)S(1)}, u32[]{:S(2)}, u32[]{:S(2)}) collective-permute-start(bf16[256,512]{1,0:T(8,128)(2,1)S(1)} %get-tuple-element.7), channel_id=1, source_target_pairs={{0,4},{2,6},{4,0},{6,2},{1,5},{3,7},{5,1},{7,3},{8,12},{10,14},{12... | collective-permute-start | bytes 786440 | tf_op jit(solution)/shard_map/ppermute | solution.py:18
  108.9 3.0 %collective-permute-start.3 = (bf16[256,512]{1,0:T(8,128)(2,1)S(1)}, bf16[256,512]{1,0:T(8,128)(2,1)S(1)}, u32[]{:S(2)}, u32[]{:S(2)}) collective-permute-start(bf16[256,512]{1,0:T(8,128)(2,1)S(1)} %get-tuple-element.6), channel_id=1, source_target_pairs={{0,6},{2,0},{4,2},{6,4},{1,7},{3,1},{5,3},{7,5},{8,14},{10,8},{12,... | collective-permute-start | bytes 786440 | tf_op jit(solution)/shard_map/ppermute | solution.py:18
  111.9 3.4 %collective-permute-start.11 = (bf16[32,1024]{1,0:T(8,128)(2,1)S(1)}, bf16[32,1024]{1,0:T(8,128)(2,1)S(1)}, u32[]{:S(2)}, u32[]{:S(2)}) collective-permute-start(bf16[32,1024]{1,0:T(8,128)(2,1)S(1)} %bitcast.147), channel_id=1, source_target_pairs={{0,24},{8,0},{16,8},{24,16},{1,25},{9,1},{17,9},{25,17},{2,26},{10... | collective-permute-start | bytes 196616 | tf_op jit(solution)/shard_map/ppermute | solution.py:18
  115.3 1.6 collective-permute-done.2
  117.0 3.8 %collective-permute-done.3 = bf16[256,512]{1,0:T(8,128)(2,1)S(1)} collective-permute-done((bf16[256,512]{1,0:T(8,128)(2,1)S(1)}, bf16[256,512]{1,0:T(8,128)(2,1)S(1)}, u32[]{:S(2)}, u32[]{:S(2)}) %collective-permute-start.3) | collective-permute-done | bytes 262176 | tf_op jit(solution)/shard_map/ppermute | solution.py:18
  120.8 0.9 fusion.10
  121.7 3.8 %all-to-all-start.1 = ((f32[4,64,512]{2,1,0:T(8,128)}), f32[4,64,512]{2,1,0:T(8,128)S(1)}, u32[]{:S(2)}, u32[]{:S(2)}) async-start(f32[4,64,512]{2,1,0:T(8,128)} %bitcast.23), calls=%async_computation.1 | async-start | bytes 1048576 | tf_op jit(solution)/shard_map/all_to_all | solution.py:13
  125.5 3.8 %collective-permute-start.12 = (bf16[4,32,1024]{2,1,0:T(8,128)(2,1)S(1)}, bf16[4,32,1024]{2,1,0:T(8,128)(2,1)S(1)}, u32[]{:S(2)}, u32[]{:S(2)}) collective-permute-start(bf16[4,32,1024]{2,1,0:T(8,128)(2,1)S(1)} %bitcast_dynamic-update-slice_fusion.8), channel_id=1, source_target_pairs={{0,2},{2,4},{4,6},{6,0},{1,3},{3,5},{5,7},{7,1},{8,10},{10,12},{12... | collective-permute-start | bytes 786440 | tf_op jit(solution)/shard_map/ppermute | solution.py:18
  129.3 4.6 %collective-permute-start.13 = (bf16[4,32,1024]{2,1,0:T(8,128)(2,1)S(1)}, bf16[4,32,1024]{2,1,0:T(8,128)(2,1)S(1)}, u32[]{:S(2)}, u32[]{:S(2)}) collective-permute-start(bf16[4,32,1024]{2,1,0:T(8,128)(2,1)S(1)} %bitcast_dynamic-update-slice_fusion.8), channel_id=1, source_target_pairs={{0,4},{2,6},{4,0},{6,2},{1,5},{3,7},{5,1},{7,3},{8,12},{10,14},{12... | collective-permute-start | bytes 786440 | tf_op jit(solution)/shard_map/ppermute | solution.py:18
  133.9 1.9 collective-permute-start.14
  135.9 0.1 broadcast_in_dim.109
  136.1 5.9 %collective-permute-done.13 = bf16[4,32,1024]{2,1,0:T(8,128)(2,1)S(1)} collective-permute-done((bf16[4,32,1024]{2,1,0:T(8,128)(2,1)S(1)}, bf16[4,32,1024]{2,1,0:T(8,128)(2,1)S(1)}, u32[]{:S(2)}, u32[]{:S(2)}) %collective-permute-start.13) | collective-permute-done | bytes 262176 | tf_op jit(solution)/shard_map/ppermute | solution.py:18
  142.0 0.7 broadcast_in_dim.104
  142.7 6.4 %all-to-all-start.2 = ((bf16[4,64,512]{2,1,0:T(8,128)(2,1)}), bf16[4,64,512]{2,1,0:T(8,128)(2,1)S(1)}, u32[]{:S(2)}, u32[]{:S(2)}) async-start(bf16[4,64,512]{2,1,0:T(8,128)(2,1)} %broadcast_in_dim.104), calls=%async_computation.2 | async-start | bytes 524288 | tf_op jit(solution)/shard_map/all_to_all | solution.py:13
  149.1 1.0 bitcast_dynamic-update-slice_fusion
  150.1 1.0 copy-done.3
  151.0 2.1 fusion.6
  153.2 3.9 %all-to-all-done.2 = bf16[4,64,512]{2,1,0:T(8,128)(2,1)S(1)} async-done(((bf16[4,64,512]{2,1,0:T(8,128)(2,1)}), bf16[4,64,512]{2,1,0:T(8,128)(2,1)S(1)}, u32[]{:S(2)}, u32[]{:S(2)}) %all-to-all-start.2) | async-done | bytes 262176 | tf_op jit(solution)/shard_map/all_to_all | solution.py:13
  157.0 1.9 collective-permute-start.4
  158.9 1.8 fusion.3
  160.7 0.3 copy.32
  161.0 1.3 copy.27
  162.3 14.4 %all-to-all-start.4 = ((bf16[256,2,8,128]{3,2,1,0:T(8,128)(2,1)}), bf16[256,2,8,128]{3,2,1,0:T(8,128)(2,1)S(1)}, u32[]{:S(2)}, u32[]{:S(2)}) async-start(bf16[256,2,8,128]{3,2,1,0:T(8,128)(2,1)} %bitcast.42), calls=%async_computation.4 | async-start | bytes 2097152 | tf_op jit(solution)/shard_map/all_to_all | solution.py:13
  176.7 3.2 %collective-permute-start.5 = (bf16[256,512]{1,0:T(8,128)(2,1)S(1)}, bf16[256,512]{1,0:T(8,128)(2,1)S(1)}, u32[]{:S(2)}, u32[]{:S(2)}) collective-permute-start(bf16[256,512]{1,0:T(8,128)(2,1)S(1)} %bitcast.138), channel_id=1, source_target_pairs={{0,4},{2,6},{4,0},{6,2},{1,5},{3,7},{5,1},{7,3},{8,12},{10,14},{12... | collective-permute-start | bytes 786440 | tf_op jit(solution)/shard_map/ppermute | solution.py:18
  180.0 2.8 %collective-permute-start.6 = (bf16[256,512]{1,0:T(8,128)(2,1)S(1)}, bf16[256,512]{1,0:T(8,128)(2,1)S(1)}, u32[]{:S(2)}, u32[]{:S(2)}) collective-permute-start(bf16[256,512]{1,0:T(8,128)(2,1)S(1)} %bitcast.139), channel_id=1, source_target_pairs={{0,6},{2,0},{4,2},{6,4},{1,7},{3,1},{5,3},{7,5},{8,14},{10,8},{12,... | collective-permute-start | bytes 786440 | tf_op jit(solution)/shard_map/ppermute | solution.py:18
  182.8 0.1 broadcast_in_dim.102
  182.9 1.0 bitcast_dynamic-update-slice_fusion.6
  183.9 5.7 %collective-permute-done.5 = bf16[256,512]{1,0:T(8,128)(2,1)S(1)} collective-permute-done((bf16[256,512]{1,0:T(8,128)(2,1)S(1)}, bf16[256,512]{1,0:T(8,128)(2,1)S(1)}, u32[]{:S(2)}, u32[]{:S(2)}) %collective-permute-start.5) | collective-permute-done | bytes 262176 | tf_op jit(solution)/shard_map/ppermute | solution.py:18
  189.6 10.3 %collective-permute-done.6 = bf16[256,512]{1,0:T(8,128)(2,1)S(1)} collective-permute-done((bf16[256,512]{1,0:T(8,128)(2,1)S(1)}, bf16[256,512]{1,0:T(8,128)(2,1)S(1)}, u32[]{:S(2)}, u32[]{:S(2)}) %collective-permute-start.6) | collective-permute-done | bytes 262176 | tf_op jit(solution)/shard_map/ppermute | solution.py:18
  199.9 4.3 %collective-permute-start.7 = (bf16[1024,512]{1,0:T(8,128)(2,1)S(1)}, bf16[1024,512]{1,0:T(8,128)(2,1)}, u32[]{:S(2)}, u32[]{:S(2)}) collective-permute-start(bf16[1024,512]{1,0:T(8,128)(2,1)S(1)} %bitcast.141), channel_id=1, source_target_pairs={{0,1},{1,0},{2,3},{3,2},{4,5},{5,4},{6,7},{7,6},{8,9},{9,8},{10,11... | collective-permute-start | bytes 3145736 | tf_op jit(solution)/shard_map/ppermute | solution.py:18
  204.3 0.7 dynamic_slice.33
  205.0 0.1 dynamic_slice.32
  205.0 1.3 fusion.31
  206.4 0.2 fusion.30
  206.5 1.9 collective-permute-start.8
  208.5 0.7 broadcast_add_fusion
  209.3 0.2 select_reduce_fusion
  209.5 0.8 collective-permute-done.8
  210.4 1.9 fusion.34
  212.3 0.3 copy.28
  212.6 0.8 copy-done.5
  213.3 0.3 copy-done.9
  213.7 1.8 divide_convert_fusion
  (63 shorter events, 0.6 us)
Async XLA Ops:
  0.0 25.9 %copy-start = (bf16[2,1024]{1,0:T(2,128)(2,1)S(1)}, bf16[2,1024]{1,0:T(2,128)(2,1)}, u32[]{:S(2)}) copy-start(bf16[2,1024]{1,0:T(2,128)(2,1)} %param.9) | copy-start | bytes 12292
  2.5 24.2 %copy-start.10 = (bf16[512,64]{0,1:T(8,128)(2,1)S(1)}, bf16[512,64]{0,1:T(8,128)(2,1)}, u32[]{:S(2)}) copy-start(bf16[512,64]{0,1:T(8,128)(2,1)} %param.8) | copy-start | bytes 196612
  2.5 52.9 %all-to-all-start.3 = ((bf16[256,2,8,128]{3,2,1,0:T(8,128)(2,1)}), bf16[256,2,8,128]{3,2,1,0:T(8,128)(2,1)S(1)}, u32[]{:S(2)}, u32[]{:S(2)}) async-start(bf16[256,2,8,128]{3,2,1,0:T(8,128)(2,1)} %bitcast.40), calls=%async_computation.3 | async-start | bytes 2097152 | tf_op jit(solution)/shard_map/all_to_all | solution.py:13
  25.9 36.9 %copy-start.1 = (bf16[1024,512]{1,0:T(8,128)(2,1)S(1)}, bf16[1024,512]{1,0:T(8,128)(2,1)}, u32[]{:S(2)}) copy-start(bf16[1024,512]{1,0:T(8,128)(2,1)} %param.7) | copy-start | bytes 3145732
  56.6 35.6 %all-to-all-start = ((bf16[32,17,8,128]{3,2,1,0:T(8,128)(2,1)}), bf16[32,17,8,128]{3,2,1,0:T(8,128)(2,1)S(1)}, u32[]{:S(2)}, u32[]{:S(2)}) async-start(bf16[32,17,8,128]{3,2,1,0:T(8,128)(2,1)} %bitcast.122), calls=%async_computation | async-start | bytes 2228224 | tf_op jit(solution)/shard_map/all_to_all | solution.py:13
  64.5 1.6 copy-start.2
  66.7 34.2 %collective-permute-start = (bf16[1024,512]{1,0:T(8,128)(2,1)S(1)}, bf16[1024,512]{1,0:T(8,128)(2,1)}, u32[]{:S(2)}, u32[]{:S(2)}) collective-permute-start(bf16[1024,512]{1,0:T(8,128)(2,1)S(1)} %bitcast.123), channel_id=1, source_target_pairs={{0,1},{1,0},{2,3},{3,2},{4,5},{5,4},{6,7},{7,6},{8,9},{9,8},{10,11... | collective-permute-start | bytes 3145736 | tf_op jit(solution)/shard_map/ppermute | solution.py:18
  70.3 79.7 %collective-permute-start.15 = (bf16[512,1024]{1,0:T(8,128)(2,1)}, bf16[512,1024]{1,0:T(8,128)(2,1)}, u32[]{:S(2)}, u32[]{:S(2)}) collective-permute-start(bf16[512,1024]{1,0:T(8,128)(2,1)} %bitcast.111), channel_id=1, source_target_pairs={{0,1},{1,0},{2,3},{3,2},{4,5},{5,4},{6,7},{7,6},{8,9},{9,8},{10,11... | collective-permute-start | bytes 3145736 | tf_op jit(solution)/shard_map/ppermute | solution.py:18
  92.3 16.6 %collective-permute-start.9 = (bf16[32,1024]{1,0:T(8,128)(2,1)S(1)}, bf16[32,1024]{1,0:T(8,128)(2,1)S(1)}, u32[]{:S(2)}, u32[]{:S(2)}) collective-permute-start(bf16[32,1024]{1,0:T(8,128)(2,1)S(1)} %bitcast.145), channel_id=1, source_target_pairs={{0,8},{8,16},{16,24},{24,0},{1,9},{9,17},{17,25},{25,1},{2,10},{10... | collective-permute-start | bytes 196616 | tf_op jit(solution)/shard_map/ppermute | solution.py:18
  95.7 16.2 %collective-permute-start.10 = (bf16[32,1024]{1,0:T(8,128)(2,1)S(1)}, bf16[32,1024]{1,0:T(8,128)(2,1)S(1)}, u32[]{:S(2)}, u32[]{:S(2)}) collective-permute-start(bf16[32,1024]{1,0:T(8,128)(2,1)S(1)} %bitcast.146), channel_id=1, source_target_pairs={{0,16},{8,24},{16,0},{24,8},{1,17},{9,25},{17,1},{25,9},{2,18},{10... | collective-permute-start | bytes 196616 | tf_op jit(solution)/shard_map/ppermute | solution.py:18
  100.2 0.8 copy-start.4
  100.2 2.8 %copy-start.6 = (bf16[16,1,32,512]{3,2,1,0:T(8,128)(2,1)}, bf16[16,1,32,512]{3,2,1,0:T(8,128)(2,1)S(1)}, u32[]{:S(2)}) copy-start(bf16[16,1,32,512]{3,2,1,0:T(8,128)(2,1)S(1)} %get-tuple-element.8) | copy-start | bytes 1572868
  103.0 12.3 %collective-permute-start.1 = (bf16[256,512]{1,0:T(8,128)(2,1)S(1)}, bf16[256,512]{1,0:T(8,128)(2,1)S(1)}, u32[]{:S(2)}, u32[]{:S(2)}) collective-permute-start(bf16[256,512]{1,0:T(8,128)(2,1)S(1)} %get-tuple-element.5), channel_id=1, source_target_pairs={{0,2},{2,4},{4,6},{6,0},{1,3},{3,5},{5,7},{7,1},{8,10},{10,12},{12... | collective-permute-start | bytes 786440 | tf_op jit(solution)/shard_map/ppermute | solution.py:18
  105.2 11.7 %collective-permute-start.2 = (bf16[256,512]{1,0:T(8,128)(2,1)S(1)}, bf16[256,512]{1,0:T(8,128)(2,1)S(1)}, u32[]{:S(2)}, u32[]{:S(2)}) collective-permute-start(bf16[256,512]{1,0:T(8,128)(2,1)S(1)} %get-tuple-element.7), channel_id=1, source_target_pairs={{0,4},{2,6},{4,0},{6,2},{1,5},{3,7},{5,1},{7,3},{8,12},{10,14},{12... | collective-permute-start | bytes 786440 | tf_op jit(solution)/shard_map/ppermute | solution.py:18
  108.9 11.9 %collective-permute-start.3 = (bf16[256,512]{1,0:T(8,128)(2,1)S(1)}, bf16[256,512]{1,0:T(8,128)(2,1)S(1)}, u32[]{:S(2)}, u32[]{:S(2)}) collective-permute-start(bf16[256,512]{1,0:T(8,128)(2,1)S(1)} %get-tuple-element.6), channel_id=1, source_target_pairs={{0,6},{2,0},{4,2},{6,4},{1,7},{3,1},{5,3},{7,5},{8,14},{10,8},{12,... | collective-permute-start | bytes 786440 | tf_op jit(solution)/shard_map/ppermute | solution.py:18
  111.9 13.5 %collective-permute-start.11 = (bf16[32,1024]{1,0:T(8,128)(2,1)S(1)}, bf16[32,1024]{1,0:T(8,128)(2,1)S(1)}, u32[]{:S(2)}, u32[]{:S(2)}) collective-permute-start(bf16[32,1024]{1,0:T(8,128)(2,1)S(1)} %bitcast.147), channel_id=1, source_target_pairs={{0,24},{8,0},{16,8},{24,16},{1,25},{9,1},{17,9},{25,17},{2,26},{10... | collective-permute-start | bytes 196616 | tf_op jit(solution)/shard_map/ppermute | solution.py:18
  121.7 20.3 %all-to-all-start.1 = ((f32[4,64,512]{2,1,0:T(8,128)}), f32[4,64,512]{2,1,0:T(8,128)S(1)}, u32[]{:S(2)}, u32[]{:S(2)}) async-start(f32[4,64,512]{2,1,0:T(8,128)} %bitcast.23), calls=%async_computation.1 | async-start | bytes 1048576 | tf_op jit(solution)/shard_map/all_to_all | solution.py:13
  125.5 10.6 %collective-permute-start.12 = (bf16[4,32,1024]{2,1,0:T(8,128)(2,1)S(1)}, bf16[4,32,1024]{2,1,0:T(8,128)(2,1)S(1)}, u32[]{:S(2)}, u32[]{:S(2)}) collective-permute-start(bf16[4,32,1024]{2,1,0:T(8,128)(2,1)S(1)} %bitcast_dynamic-update-slice_fusion.8), channel_id=1, source_target_pairs={{0,2},{2,4},{4,6},{6,0},{1,3},{3,5},{5,7},{7,1},{8,10},{10,12},{12... | collective-permute-start | bytes 786440 | tf_op jit(solution)/shard_map/ppermute | solution.py:18
  129.3 12.6 %collective-permute-start.13 = (bf16[4,32,1024]{2,1,0:T(8,128)(2,1)S(1)}, bf16[4,32,1024]{2,1,0:T(8,128)(2,1)S(1)}, u32[]{:S(2)}, u32[]{:S(2)}) collective-permute-start(bf16[4,32,1024]{2,1,0:T(8,128)(2,1)S(1)} %bitcast_dynamic-update-slice_fusion.8), channel_id=1, source_target_pairs={{0,4},{2,6},{4,0},{6,2},{1,5},{3,7},{5,1},{7,3},{8,12},{10,14},{12... | collective-permute-start | bytes 786440 | tf_op jit(solution)/shard_map/ppermute | solution.py:18
  133.9 15.2 %collective-permute-start.14 = (bf16[4,32,1024]{2,1,0:T(8,128)(2,1)S(1)}, bf16[4,32,1024]{2,1,0:T(8,128)(2,1)}, u32[]{:S(2)}, u32[]{:S(2)}) collective-permute-start(bf16[4,32,1024]{2,1,0:T(8,128)(2,1)S(1)} %bitcast_dynamic-update-slice_fusion.8), channel_id=1, source_target_pairs={{0,6},{2,0},{4,2},{6,4},{1,7},{3,1},{5,3},{7,5},{8,14},{10,8},{12,... | collective-permute-start | bytes 786440 | tf_op jit(solution)/shard_map/ppermute | solution.py:18
  142.7 14.3 %all-to-all-start.2 = ((bf16[4,64,512]{2,1,0:T(8,128)(2,1)}), bf16[4,64,512]{2,1,0:T(8,128)(2,1)S(1)}, u32[]{:S(2)}, u32[]{:S(2)}) async-start(bf16[4,64,512]{2,1,0:T(8,128)(2,1)} %broadcast_in_dim.104), calls=%async_computation.2 | async-start | bytes 524288 | tf_op jit(solution)/shard_map/all_to_all | solution.py:13
  150.1 1.0 copy-start.3
  157.0 25.9 %collective-permute-start.4 = (bf16[256,512]{1,0:T(8,128)(2,1)S(1)}, bf16[256,512]{1,0:T(8,128)(2,1)}, u32[]{:S(2)}, u32[]{:S(2)}) collective-permute-start(bf16[256,512]{1,0:T(8,128)(2,1)S(1)} %bitcast.137), channel_id=1, source_target_pairs={{0,2},{2,4},{4,6},{6,0},{1,3},{3,5},{5,7},{7,1},{8,10},{10,12},{12... | collective-permute-start | bytes 786440 | tf_op jit(solution)/shard_map/ppermute | solution.py:18
  162.3 50.0 %all-to-all-start.4 = ((bf16[256,2,8,128]{3,2,1,0:T(8,128)(2,1)}), bf16[256,2,8,128]{3,2,1,0:T(8,128)(2,1)S(1)}, u32[]{:S(2)}, u32[]{:S(2)}) async-start(bf16[256,2,8,128]{3,2,1,0:T(8,128)(2,1)} %bitcast.42), calls=%async_computation.4 | async-start | bytes 2097152 | tf_op jit(solution)/shard_map/all_to_all | solution.py:13
  176.7 27.6 %copy-start.14 = (s32[32]{0:T(128)S(1)}, s32[32]{0:T(128)}, u32[]{:S(2)}) copy-start(s32[32]{0:T(128)} %param.11) | copy-start | bytes 388
  176.7 28.4 %copy-start.11 = (f32[200]{0:T(256)S(1)}, f32[200]{0:T(256)}, u32[]{:S(2)}) copy-start(f32[200]{0:T(256)} %param.10) | copy-start | bytes 2404
  176.7 29.9 %copy-start.7 = (bf16[16,1,32,512]{3,2,1,0:T(8,128)(2,1)S(1)}, bf16[16,1,32,512]{3,2,1,0:T(8,128)(2,1)}, u32[]{:S(2)}) copy-start(bf16[16,1,32,512]{3,2,1,0:T(8,128)(2,1)} %copy-done.6) | copy-start | bytes 1572868
  176.7 32.6 %copy-start.12 = (f32[512]{0:T(512)S(1)}, f32[512]{0:T(512)}, u32[]{:S(2)}) copy-start(f32[512]{0:T(512)} %param.12) | copy-start | bytes 6148
  176.7 32.5 %copy-start.13 = (s32[512]{0:T(512)S(1)}, s32[512]{0:T(512)}, u32[]{:S(2)}) copy-start(s32[512]{0:T(512)} %param.13) | copy-start | bytes 6148
  176.7 12.9 %collective-permute-start.5 = (bf16[256,512]{1,0:T(8,128)(2,1)S(1)}, bf16[256,512]{1,0:T(8,128)(2,1)S(1)}, u32[]{:S(2)}, u32[]{:S(2)}) collective-permute-start(bf16[256,512]{1,0:T(8,128)(2,1)S(1)} %bitcast.138), channel_id=1, source_target_pairs={{0,4},{2,6},{4,0},{6,2},{1,5},{3,7},{5,1},{7,3},{8,12},{10,14},{12... | collective-permute-start | bytes 786440 | tf_op jit(solution)/shard_map/ppermute | solution.py:18
  180.0 19.9 %collective-permute-start.6 = (bf16[256,512]{1,0:T(8,128)(2,1)S(1)}, bf16[256,512]{1,0:T(8,128)(2,1)S(1)}, u32[]{:S(2)}, u32[]{:S(2)}) collective-permute-start(bf16[256,512]{1,0:T(8,128)(2,1)S(1)} %bitcast.139), channel_id=1, source_target_pairs={{0,6},{2,0},{4,2},{6,4},{1,7},{3,1},{5,3},{7,5},{8,14},{10,8},{12,... | collective-permute-start | bytes 786440 | tf_op jit(solution)/shard_map/ppermute | solution.py:18
  199.9 10.4 %copy-start.8 = (bf16[4,256,512]{2,1,0:T(8,128)(2,1)}, bf16[4,256,512]{2,1,0:T(8,128)(2,1)S(1)}, u32[]{:S(2)}) copy-start(bf16[4,256,512]{2,1,0:T(8,128)(2,1)S(1)} %bitcast_dynamic-update-slice_fusion.4) | copy-start | bytes 3145732
  199.9 10.4 %collective-permute-start.7 = (bf16[1024,512]{1,0:T(8,128)(2,1)S(1)}, bf16[1024,512]{1,0:T(8,128)(2,1)}, u32[]{:S(2)}, u32[]{:S(2)}) collective-permute-start(bf16[1024,512]{1,0:T(8,128)(2,1)S(1)} %bitcast.141), channel_id=1, source_target_pairs={{0,1},{1,0},{2,3},{3,2},{4,5},{5,4},{6,7},{7,6},{8,9},{9,8},{10,11... | collective-permute-start | bytes 3145736 | tf_op jit(solution)/shard_map/ppermute | solution.py:18
  206.5 3.8 %collective-permute-start.8 = (bf16[512,512]{1,0:T(8,128)(2,1)S(1)}, bf16[512,512]{1,0:T(8,128)(2,1)S(1)}, u32[]{:S(2)}, u32[]{:S(2)}) collective-permute-start(bf16[512,512]{1,0:T(8,128)(2,1)S(1)} %bitcast.136), channel_id=1, source_target_pairs={{0,1},{1,0},{2,3},{3,2},{4,5},{5,4},{6,7},{7,6},{8,9},{9,8},{10,11... | collective-permute-start | bytes 1572872 | tf_op jit(solution)/shard_map/ppermute | solution.py:18
  212.3 1.0 copy-start.5
  212.3 1.4 copy-start.9

commit v3 on v2

--- a/solution.py
+++ b/solution.py
@@ -69,15 +69,24 @@
     swapped = jnp.concatenate([rows[1:, 512:], rows[1:, :512]], axis=1)
     rows = jnp.concatenate([rows[:1], swapped]).reshape(2, 1, 8, 128)
     send = jnp.concatenate([tall, rows], axis=1)
-    send = jnp.broadcast_to(send[None], (16, 2, 17, 8, 128)).reshape(32, 17, 8, 128)
-    arrived = exchange(send, ("y", "zl", "core"))
-    factors = arrived[:, :16].reshape(16, 2, 4, 4, 8, 128).transpose(0, 1, 2, 4, 3, 5).reshape(16, 2, 32, 512)
-    own = lax.dynamic_index_in_dim(factors, core, 1, keepdims=False).reshape(512, 512)
-    other = lax.dynamic_index_in_dim(factors, 1 - core, 1, keepdims=False).reshape(512, 512)
+    send = jnp.broadcast_to(send[None], (8, 2, 17, 8, 128)).reshape(16, 17, 8, 128)
+    near = exchange(send, ("y", "core"))
+    far = shifted(near, "zl", 1)
 
+    def half_of(arrived, which):
+        tiles = lax.dynamic_index_in_dim(arrived.reshape(8, 2, 17, 8, 128), which, 1, keepdims=False)[:, :16]
+        return tiles.reshape(8, 4, 4, 8, 128).transpose(0, 1, 3, 2, 4).reshape(256, 512)
+
+    own = jnp.concatenate([half_of(near, core), half_of(far, core)])
+    other = jnp.concatenate([half_of(near, 1 - core), half_of(far, 1 - core)])
     tiles = amplitudes.reshape(2, 64, 8, 4, 128).transpose(1, 3, 0, 2, 4).reshape(256, 2, 8, 128)
     pairs = exchange(tiles, CHIPS)
-    weights = gather_ring(arrived[:, 16].reshape(32, 1024), "zh")
+    near_rows = gather_ring(near[:, 16].reshape(16, 1024), "zh")
+    far_rows = shifted(near_rows, "zl", 1)
+    first = lax.axis_index("zl") == 0
+    weights = jnp.stack(
+        [jnp.where(first, near_rows, far_rows), jnp.where(first, far_rows, near_rows)], axis=1
+    ).reshape(4, 32, 1024)
     weights = gather_ring(weights, "x")
     weights = weights.reshape(512, 1024)
 
@@ -98,7 +107,7 @@
     pairs = pairs.reshape(512, 1024)
     pairs_other = partner(pairs)
     hole = (dot(weights[:, :512], pairs, 1, 0) + dot(weights[:, 512:], pairs_other, 1, 0)).astype(BF)
-    hole = hole.reshape(4, 2, 2, 16, 2, 8, 128).transpose(3, 2, 0, 4, 1, 5, 6).reshape(256, 2, 8, 128)
+    hole = hole.reshape(4, 2, 2, 2, 8, 2, 8, 128).transpose(4, 3, 2, 0, 5, 1, 6, 7).reshape(256, 2, 8, 128)
     hole = exchange(hole, CHIPS)
     hole = hole.reshape(64, 4, 2, 8, 128).transpose(2, 0, 3, 1, 4).reshape(2, VIR, VIR)
 

time: 217 us -> 204 us (0.940)
  the two profiles are of different devices: /device:TPU:1 before, /device:TPU:2 now
where the time goes in v3:
time: 204 us; the launch traced here: 202 us
  starting transfers between devices  125 us (61%)
  waiting for transfers between devices  40.7 us (20%)
  local copies, waits for them, and re-layouts  17.2 us (8%)
  matrix products  11.2 us (5%)
  other arithmetic  6.64 us (3%)
    ppermute x18, starting transfers between devices, shifted(): lax.ppermute(value, axis, [(i, (i + step) % count) for i in range(count)])  69.2 us
    all_to_all x5, starting transfers between devices, exchange(): return lax.all_to_all(value, axes, split_axis=0, concat_axis=0, tiled=True)  56.3 us
    all_to_all x5, waiting for transfers between devices, exchange(): return lax.all_to_all(value, axes, split_axis=0, concat_axis=0, tiled=True)  38.7 us
    dot_general x7, matrix products, dot(): lax.dot_general(a, b, (((ca,), (cb,)), ((), ())), preferred_element_type=...  11.2 us
    dynamic_update_slice x12, local copies, waits for them, and re-layouts, gather_ring(): lax.dynamic_update_index_in_dim(everyone, near, (me - step) % count, 0)  5.92 us
  transfers between devices with their start and end apart: 23, of which 6 were waited for; matrix products, arithmetic and copies ran while one was open for 14% of the time, Pallas kernels for 0%

profile of v3, /device:TPU:2, one launch (start us, length us, event | category | flops | bytes accessed | tf_op | source)
XLA Modules:
  0.0 202.1 jit_solution(14250270556977829643)
XLA Ops:
  0.0 0.7 copy-done
  0.7 0.7 fusion.5
  1.5 0.9 pad_maximum_fusion.5
  2.3 0.9 broadcast_in_dim.103
  3.2 7.2 %all-to-all-start = ((bf16[16,17,8,128]{3,2,1,0:T(8,128)(2,1)}), bf16[16,17,8,128]{3,2,1,0:T(8,128)(2,1)}, u32[]{:S(2)}, u32[]{:S(2)}) async-start(bf16[16,17,8,128]{3,2,1,0:T(8,128)(2,1)} %bitcast.10), calls=%async_computation | async-start | bytes 1114112 | tf_op jit(solution)/shard_map/all_to_all | solution.py:13
  10.5 0.5 copy.44
  11.0 0.3 broadcast_multiply_fusion
  11.3 1.4 fusion.1
  12.8 2.3 %collective-permute-start.1 = (bf16[1024,512]{1,0:T(8,128)(2,1)}, bf16[1024,512]{1,0:T(8,128)(2,1)}, u32[]{:S(2)}, u32[]{:S(2)}) collective-permute-start(bf16[1024,512]{1,0:T(8,128)(2,1)} %bitcast.3), channel_id=1, source_target_pairs={{0,1},{1,0},{2,3},{3,2},{4,5},{5,4},{6,7},{7,6},{8,9},{9,8},{10,11... | collective-permute-start | bytes 3145736 | tf_op jit(solution)/shard_map/ppermute | solution.py:18
  15.0 12.1 %all-to-all-done = bf16[16,17,8,128]{3,2,1,0:T(8,128)(2,1)} async-done(((bf16[16,17,8,128]{3,2,1,0:T(8,128)(2,1)}), bf16[16,17,8,128]{3,2,1,0:T(8,128)(2,1)}, u32[]{:S(2)}, u32[]{:S(2)}) %all-to-all-start) | async-done | bytes 557088 | tf_op jit(solution)/shard_map/all_to_all | solution.py:13
  27.1 4.3 %collective-permute-start = (bf16[16,17,8,128]{3,2,1,0:T(8,128)(2,1)}, bf16[16,17,8,128]{3,2,1,0:T(8,128)(2,1)S(1)}, u32[]{:S(2)}, u32[]{:S(2)}) collective-permute-start(bf16[16,17,8,128]{3,2,1,0:T(8,128)(2,1)} %all-to-all-done), channel_id=1, source_target_pairs={{0,32},{32,0},{1,33},{33,1},{2,34},{34,2},{3,35},{35,3},{4,36},{36... | collective-permute-start | bytes 1671176 | tf_op jit(solution)/shard_map/ppermute | solution.py:18
  31.3 1.3 copy.47
  32.6 17.6 %all-to-all-start.3 = ((bf16[256,2,8,128]{3,2,1,0:T(8,128)(2,1)}), bf16[256,2,8,128]{3,2,1,0:T(8,128)(2,1)S(1)}, u32[]{:S(2)}, u32[]{:S(2)}) async-start(bf16[256,2,8,128]{3,2,1,0:T(8,128)(2,1)} %bitcast.55), calls=%async_computation.3 | async-start | bytes 2097152 | tf_op jit(solution)/shard_map/all_to_all | solution.py:13
  50.4 0.8 slice.47
  51.2 4.3 %collective-permute-start.10 = (bf16[16,1024]{1,0:T(8,128)(2,1)S(1)}, bf16[16,1024]{1,0:T(8,128)(2,1)S(1)}, u32[]{:S(2)}, u32[]{:S(2)}) collective-permute-start(bf16[16,1024]{1,0:T(8,128)(2,1)S(1)} %bitcast.172), channel_id=1, source_target_pairs={{0,8},{8,16},{16,24},{24,0},{1,9},{9,17},{17,25},{25,1},{2,10},{10... | collective-permute-start | bytes 98312 | tf_op jit(solution)/shard_map/ppermute | solution.py:18
  55.5 5.5 %collective-permute-start.11 = (bf16[16,1024]{1,0:T(8,128)(2,1)S(1)}, bf16[16,1024]{1,0:T(8,128)(2,1)S(1)}, u32[]{:S(2)}, u32[]{:S(2)}) collective-permute-start(bf16[16,1024]{1,0:T(8,128)(2,1)S(1)} %bitcast.173), channel_id=1, source_target_pairs={{0,16},{8,24},{16,0},{24,8},{1,17},{9,25},{17,1},{25,9},{2,18},{10... | collective-permute-start | bytes 98312 | tf_op jit(solution)/shard_map/ppermute | solution.py:18
  61.0 5.5 %collective-permute-start.12 = (bf16[16,1024]{1,0:T(8,128)(2,1)S(1)}, bf16[16,1024]{1,0:T(8,128)(2,1)S(1)}, u32[]{:S(2)}, u32[]{:S(2)}) collective-permute-start(bf16[16,1024]{1,0:T(8,128)(2,1)S(1)} %bitcast.174), channel_id=1, source_target_pairs={{0,24},{8,0},{16,8},{24,16},{1,25},{9,1},{17,9},{25,17},{2,26},{10... | collective-permute-start | bytes 98312 | tf_op jit(solution)/shard_map/ppermute | solution.py:18
  66.5 1.1 dynamic-slice_bitcast_fusion.1
  67.7 1.2 collective-permute-done.10
  69.0 2.0 %fusion.11 = f32[1024,512]{1,0:T(8,128)S(1)} fusion(bf16[1024,512]{1,0:T(8,128)(2,1)} %bitcast.3, bf16[256,512]{1,0:T(8,128)(2,1)S(1)} %bitcast.161, bf16[256,512]{1,0:T(8,128)(2,1)S(1)} %bitcast.159), kind=kOutput, calls=%fused_computation.23 | convolution fusion | flops 537919488 | bytes 3670016 | tf_op jit(solution)/shard_map/dot_general | solution.py:57
  71.1 2.0 add_convert_fusion.1
  73.2 3.6 %collective-permute-start.2 = (bf16[256,512]{1,0:T(8,128)(2,1)S(1)}, bf16[256,512]{1,0:T(8,128)(2,1)S(1)}, u32[]{:S(2)}, u32[]{:S(2)}) collective-permute-start(bf16[256,512]{1,0:T(8,128)(2,1)S(1)} %get-tuple-element.5), channel_id=1, source_target_pairs={{0,2},{2,4},{4,6},{6,0},{1,3},{3,5},{5,7},{7,1},{8,10},{10,12},{12... | collective-permute-start | bytes 786440 | tf_op jit(solution)/shard_map/ppermute | solution.py:18
  76.8 6.2 %collective-permute-start.3 = (bf16[256,512]{1,0:T(8,128)(2,1)S(1)}, bf16[256,512]{1,0:T(8,128)(2,1)S(1)}, u32[]{:S(2)}, u32[]{:S(2)}) collective-permute-start(bf16[256,512]{1,0:T(8,128)(2,1)S(1)} %get-tuple-element.7), channel_id=1, source_target_pairs={{0,4},{2,6},{4,0},{6,2},{1,5},{3,7},{5,1},{7,3},{8,12},{10,14},{12... | collective-permute-start | bytes 786440 | tf_op jit(solution)/shard_map/ppermute | solution.py:18
  83.0 1.9 collective-permute-start.4
  84.9 8.8 %collective-permute-start.13 = (bf16[4,16,1024]{2,1,0:T(8,128)(2,1)S(1)}, bf16[4,16,1024]{2,1,0:T(8,128)(2,1)S(1)}, u32[]{:S(2)}, u32[]{:S(2)}) collective-permute-start(bf16[4,16,1024]{2,1,0:T(8,128)(2,1)S(1)} %bitcast_dynamic-update-slice_fusion.7), channel_id=1, source_target_pairs={{0,32},{32,0},{1,33},{33,1},{2,34},{34,2},{3,35},{35,3},{4,36},{36... | collective-permute-start | bytes 393224 | tf_op jit(solution)/shard_map/ppermute | solution.py:18
  93.9 0.9 fusion.10
  94.9 7.1 %all-to-all-start.1 = ((f32[4,64,512]{2,1,0:T(8,128)}), f32[4,64,512]{2,1,0:T(8,128)S(1)}, u32[]{:S(2)}, u32[]{:S(2)}) async-start(f32[4,64,512]{2,1,0:T(8,128)} %bitcast.34), calls=%async_computation.1 | async-start | bytes 1048576 | tf_op jit(solution)/shard_map/all_to_all | solution.py:13
  102.0 1.2 copy.59
  103.2 1.9 collective-permute-start.17
  105.1 0.8 pad_maximum_fusion.4
  105.9 2.5 %collective-permute-start.14 = (bf16[4,32,1024]{2,1,0:T(8,128)(2,1)}, bf16[4,32,1024]{2,1,0:T(8,128)(2,1)}, u32[]{:S(2)}, u32[]{:S(2)}) collective-permute-start(bf16[4,32,1024]{2,1,0:T(8,128)(2,1)} %bitcast.48), channel_id=1, source_target_pairs={{0,2},{2,4},{4,6},{6,0},{1,3},{3,5},{5,7},{7,1},{8,10},{10,12},{12... | collective-permute-start | bytes 786440 | tf_op jit(solution)/shard_map/ppermute | solution.py:18
  108.4 4.5 %collective-permute-start.15 = (bf16[4,32,1024]{2,1,0:T(8,128)(2,1)}, bf16[4,32,1024]{2,1,0:T(8,128)(2,1)}, u32[]{:S(2)}, u32[]{:S(2)}) collective-permute-start(bf16[4,32,1024]{2,1,0:T(8,128)(2,1)} %bitcast.48), channel_id=1, source_target_pairs={{0,4},{2,6},{4,0},{6,2},{1,5},{3,7},{5,1},{7,3},{8,12},{10,14},{12... | collective-permute-start | bytes 786440 | tf_op jit(solution)/shard_map/ppermute | solution.py:18
  113.0 4.0 %collective-permute-start.16 = (bf16[4,32,1024]{2,1,0:T(8,128)(2,1)}, bf16[4,32,1024]{2,1,0:T(8,128)(2,1)}, u32[]{:S(2)}, u32[]{:S(2)}) collective-permute-start(bf16[4,32,1024]{2,1,0:T(8,128)(2,1)} %bitcast.48), channel_id=1, source_target_pairs={{0,6},{2,0},{4,2},{6,4},{1,7},{3,1},{5,3},{7,5},{8,14},{10,8},{12,... | collective-permute-start | bytes 786440 | tf_op jit(solution)/shard_map/ppermute | solution.py:18
  117.1 1.0 constant_dynamic-update-slice_fusion
  118.1 1.0 bitcast_dynamic-update-slice_fusion.2
  119.1 0.7 broadcast_in_dim.104
  119.9 7.2 %all-to-all-start.2 = ((bf16[4,64,512]{2,1,0:T(8,128)(2,1)}), bf16[4,64,512]{2,1,0:T(8,128)(2,1)S(1)}, u32[]{:S(2)}, u32[]{:S(2)}) async-start(bf16[4,64,512]{2,1,0:T(8,128)(2,1)} %broadcast_in_dim.104), calls=%async_computation.2 | async-start | bytes 524288 | tf_op jit(solution)/shard_map/all_to_all | solution.py:13
  127.1 1.0 bitcast_dynamic-update-slice_fusion.1
  128.0 1.0 bitcast_dynamic-update-slice_fusion
  129.0 9.0 %all-to-all-done.2 = bf16[4,64,512]{2,1,0:T(8,128)(2,1)S(1)} async-done(((bf16[4,64,512]{2,1,0:T(8,128)(2,1)}), bf16[4,64,512]{2,1,0:T(8,128)(2,1)S(1)}, u32[]{:S(2)}, u32[]{:S(2)}) %all-to-all-start.2) | async-done | bytes 262176 | tf_op jit(solution)/shard_map/all_to_all | solution.py:13
  138.1 1.9 collective-permute-start.5
  140.0 5.0 %collective-permute-start.6 = (bf16[256,512]{1,0:T(8,128)(2,1)S(1)}, bf16[256,512]{1,0:T(8,128)(2,1)}, u32[]{:S(2)}, u32[]{:S(2)}) collective-permute-start(bf16[256,512]{1,0:T(8,128)(2,1)S(1)} %bitcast.164), channel_id=1, source_target_pairs={{0,4},{2,6},{4,0},{6,2},{1,5},{3,7},{5,1},{7,3},{8,12},{10,14},{12... | collective-permute-start | bytes 786440 | tf_op jit(solution)/shard_map/ppermute | solution.py:18
  145.0 2.8 %collective-permute-start.7 = (bf16[256,512]{1,0:T(8,128)(2,1)S(1)}, bf16[256,512]{1,0:T(8,128)(2,1)S(1)}, u32[]{:S(2)}, u32[]{:S(2)}) collective-permute-start(bf16[256,512]{1,0:T(8,128)(2,1)S(1)} %bitcast.165), channel_id=1, source_target_pairs={{0,6},{2,0},{4,2},{6,4},{1,7},{3,1},{5,3},{7,5},{8,14},{10,8},{12,... | collective-permute-start | bytes 786440 | tf_op jit(solution)/shard_map/ppermute | solution.py:18
  147.8 1.9 fusion.6
  149.7 0.7 fusion.3
  150.4 0.3 copy.53
  150.7 1.3 copy.48
  152.0 17.1 %all-to-all-start.4 = ((bf16[256,2,8,128]{3,2,1,0:T(8,128)(2,1)}), bf16[256,2,8,128]{3,2,1,0:T(8,128)(2,1)S(1)}, u32[]{:S(2)}, u32[]{:S(2)}) async-start(bf16[256,2,8,128]{3,2,1,0:T(8,128)(2,1)} %bitcast.57), calls=%async_computation.4 | async-start | bytes 2097152 | tf_op jit(solution)/shard_map/all_to_all | solution.py:13
  169.3 1.0 bitcast_dynamic-update-slice_fusion.5
  170.3 1.0 bitcast_dynamic-update-slice_fusion.4
  171.3 1.9 collective-permute-start.8
  173.3 0.6 dynamic_slice.41
  174.0 1.3 fusion.32
  175.3 0.2 fusion.31
  175.5 2.4 %collective-permute-start.9 = (bf16[512,512]{1,0:T(8,128)(2,1)S(1)}, bf16[512,512]{1,0:T(8,128)(2,1)S(1)}, u32[]{:S(2)}, u32[]{:S(2)}) collective-permute-start(bf16[512,512]{1,0:T(8,128)(2,1)S(1)} %pad_maximum_fusion.1), channel_id=1, source_target_pairs={{0,1},{1,0},{2,3},{3,2},{4,5},{5,4},{6,7},{7,6},{8,9},{9,8},{10,11... | collective-permute-start | bytes 1572872 | tf_op jit(solution)/shard_map/ppermute | solution.py:18
  177.9 0.6 broadcast_add_fusion
  178.5 0.2 select_reduce_fusion
  178.8 0.6 collective-permute-done.9
  179.4 1.9 fusion.36
  181.3 17.6 %all-to-all-done.4 = bf16[256,2,8,128]{3,2,1,0:T(8,128)(2,1)S(1)} async-done(((bf16[256,2,8,128]{3,2,1,0:T(8,128)(2,1)}), bf16[256,2,8,128]{3,2,1,0:T(8,128)(2,1)S(1)}, u32[]{:S(2)}, u32[]{:S(2)}) %all-to-all-start.4) | async-done | bytes 1048608 | tf_op jit(solution)/shard_map/all_to_all | solution.py:13
  198.9 0.3 copy.49
  199.2 0.7 copy-done.3
  199.9 0.4 copy-done.5
  200.2 1.9 divide_convert_fusion
  (64 shorter events, 1.1 us)
Async XLA Ops:
  0.0 0.7 copy-start
  0.0 10.5 %copy-start.1 = (bf16[1024,512]{1,0:T(8,128)(2,1)S(1)}, bf16[1024,512]{1,0:T(8,128)(2,1)}, u32[]{:S(2)}) copy-start(bf16[1024,512]{1,0:T(8,128)(2,1)} %param.7) | copy-start | bytes 3145732
  3.2 23.9 %all-to-all-start = ((bf16[16,17,8,128]{3,2,1,0:T(8,128)(2,1)}), bf16[16,17,8,128]{3,2,1,0:T(8,128)(2,1)}, u32[]{:S(2)}, u32[]{:S(2)}) async-start(bf16[16,17,8,128]{3,2,1,0:T(8,128)(2,1)} %bitcast.10), calls=%async_computation | async-start | bytes 1114112 | tf_op jit(solution)/shard_map/all_to_all | solution.py:13
  12.8 58.3 %collective-permute-start.1 = (bf16[1024,512]{1,0:T(8,128)(2,1)}, bf16[1024,512]{1,0:T(8,128)(2,1)}, u32[]{:S(2)}, u32[]{:S(2)}) collective-permute-start(bf16[1024,512]{1,0:T(8,128)(2,1)} %bitcast.3), channel_id=1, source_target_pairs={{0,1},{1,0},{2,3},{3,2},{4,5},{5,4},{6,7},{7,6},{8,9},{9,8},{10,11... | collective-permute-start | bytes 3145736 | tf_op jit(solution)/shard_map/ppermute | solution.py:18
  27.1 41.8 %collective-permute-start = (bf16[16,17,8,128]{3,2,1,0:T(8,128)(2,1)}, bf16[16,17,8,128]{3,2,1,0:T(8,128)(2,1)S(1)}, u32[]{:S(2)}, u32[]{:S(2)}) collective-permute-start(bf16[16,17,8,128]{3,2,1,0:T(8,128)(2,1)} %all-to-all-done), channel_id=1, source_target_pairs={{0,32},{32,0},{1,33},{33,1},{2,34},{34,2},{3,35},{35,3},{4,36},{36... | collective-permute-start | bytes 1671176 | tf_op jit(solution)/shard_map/ppermute | solution.py:18
  32.6 62.2 %all-to-all-start.3 = ((bf16[256,2,8,128]{3,2,1,0:T(8,128)(2,1)}), bf16[256,2,8,128]{3,2,1,0:T(8,128)(2,1)S(1)}, u32[]{:S(2)}, u32[]{:S(2)}) async-start(bf16[256,2,8,128]{3,2,1,0:T(8,128)(2,1)} %bitcast.55), calls=%async_computation.3 | async-start | bytes 2097152 | tf_op jit(solution)/shard_map/all_to_all | solution.py:13
  51.2 17.7 %collective-permute-start.10 = (bf16[16,1024]{1,0:T(8,128)(2,1)S(1)}, bf16[16,1024]{1,0:T(8,128)(2,1)S(1)}, u32[]{:S(2)}, u32[]{:S(2)}) collective-permute-start(bf16[16,1024]{1,0:T(8,128)(2,1)S(1)} %bitcast.172), channel_id=1, source_target_pairs={{0,8},{8,16},{16,24},{24,0},{1,9},{9,17},{17,25},{25,1},{2,10},{10... | collective-permute-start | bytes 98312 | tf_op jit(solution)/shard_map/ppermute | solution.py:18
  55.5 29.4 %collective-permute-start.11 = (bf16[16,1024]{1,0:T(8,128)(2,1)S(1)}, bf16[16,1024]{1,0:T(8,128)(2,1)S(1)}, u32[]{:S(2)}, u32[]{:S(2)}) collective-permute-start(bf16[16,1024]{1,0:T(8,128)(2,1)S(1)} %bitcast.173), channel_id=1, source_target_pairs={{0,16},{8,24},{16,0},{24,8},{1,17},{9,25},{17,1},{25,9},{2,18},{10... | collective-permute-start | bytes 98312 | tf_op jit(solution)/shard_map/ppermute | solution.py:18
  61.0 23.9 %collective-permute-start.12 = (bf16[16,1024]{1,0:T(8,128)(2,1)S(1)}, bf16[16,1024]{1,0:T(8,128)(2,1)S(1)}, u32[]{:S(2)}, u32[]{:S(2)}) collective-permute-start(bf16[16,1024]{1,0:T(8,128)(2,1)S(1)} %bitcast.174), channel_id=1, source_target_pairs={{0,24},{8,0},{16,8},{24,16},{1,25},{9,1},{17,9},{25,17},{2,26},{10... | collective-permute-start | bytes 98312 | tf_op jit(solution)/shard_map/ppermute | solution.py:18
  69.0 2.1 %copy-start.2 = (bf16[8,16,8,128]{3,2,1,0:T(8,128)(2,1)}, bf16[8,16,8,128]{3,2,1,0:T(8,128)(2,1)S(1)}, u32[]{:S(2)}) copy-start(bf16[8,16,8,128]{3,2,1,0:T(8,128)(2,1)S(1)} %slice.44) | copy-start | bytes 786436
  73.2 20.6 %collective-permute-start.2 = (bf16[256,512]{1,0:T(8,128)(2,1)S(1)}, bf16[256,512]{1,0:T(8,128)(2,1)S(1)}, u32[]{:S(2)}, u32[]{:S(2)}) collective-permute-start(bf16[256,512]{1,0:T(8,128)(2,1)S(1)} %get-tuple-element.5), channel_id=1, source_target_pairs={{0,2},{2,4},{4,6},{6,0},{1,3},{3,5},{5,7},{7,1},{8,10},{10,12},{12... | collective-permute-start | bytes 786440 | tf_op jit(solution)/shard_map/ppermute | solution.py:18
  76.8 17.0 %collective-permute-start.3 = (bf16[256,512]{1,0:T(8,128)(2,1)S(1)}, bf16[256,512]{1,0:T(8,128)(2,1)S(1)}, u32[]{:S(2)}, u32[]{:S(2)}) collective-permute-start(bf16[256,512]{1,0:T(8,128)(2,1)S(1)} %get-tuple-element.7), channel_id=1, source_target_pairs={{0,4},{2,6},{4,0},{6,2},{1,5},{3,7},{5,1},{7,3},{8,12},{10,14},{12... | collective-permute-start | bytes 786440 | tf_op jit(solution)/shard_map/ppermute | solution.py:18
  83.0 10.9 %collective-permute-start.4 = (bf16[256,512]{1,0:T(8,128)(2,1)S(1)}, bf16[256,512]{1,0:T(8,128)(2,1)S(1)}, u32[]{:S(2)}, u32[]{:S(2)}) collective-permute-start(bf16[256,512]{1,0:T(8,128)(2,1)S(1)} %get-tuple-element.6), channel_id=1, source_target_pairs={{0,6},{2,0},{4,2},{6,4},{1,7},{3,1},{5,3},{7,5},{8,14},{10,8},{12,... | collective-permute-start | bytes 786440 | tf_op jit(solution)/shard_map/ppermute | solution.py:18
  84.9 17.0 %collective-permute-start.13 = (bf16[4,16,1024]{2,1,0:T(8,128)(2,1)S(1)}, bf16[4,16,1024]{2,1,0:T(8,128)(2,1)S(1)}, u32[]{:S(2)}, u32[]{:S(2)}) collective-permute-start(bf16[4,16,1024]{2,1,0:T(8,128)(2,1)S(1)} %bitcast_dynamic-update-slice_fusion.7), channel_id=1, source_target_pairs={{0,32},{32,0},{1,33},{33,1},{2,34},{34,2},{3,35},{35,3},{4,36},{36... | collective-permute-start | bytes 393224 | tf_op jit(solution)/shard_map/ppermute | solution.py:18
  94.9 24.2 %all-to-all-start.1 = ((f32[4,64,512]{2,1,0:T(8,128)}), f32[4,64,512]{2,1,0:T(8,128)S(1)}, u32[]{:S(2)}, u32[]{:S(2)}) async-start(f32[4,64,512]{2,1,0:T(8,128)} %bitcast.34), calls=%async_computation.1 | async-start | bytes 1048576 | tf_op jit(solution)/shard_map/all_to_all | solution.py:13
  103.2 44.6 %collective-permute-start.17 = (bf16[512,1024]{1,0:T(8,128)(2,1)}, bf16[512,1024]{1,0:T(8,128)(2,1)}, u32[]{:S(2)}, u32[]{:S(2)}) collective-permute-start(bf16[512,1024]{1,0:T(8,128)(2,1)} %bitcast.137), channel_id=1, source_target_pairs={{0,1},{1,0},{2,3},{3,2},{4,5},{5,4},{6,7},{7,6},{8,9},{9,8},{10,11... | collective-permute-start | bytes 3145736 | tf_op jit(solution)/shard_map/ppermute | solution.py:18
  105.9 12.2 %collective-permute-start.14 = (bf16[4,32,1024]{2,1,0:T(8,128)(2,1)}, bf16[4,32,1024]{2,1,0:T(8,128)(2,1)}, u32[]{:S(2)}, u32[]{:S(2)}) collective-permute-start(bf16[4,32,1024]{2,1,0:T(8,128)(2,1)} %bitcast.48), channel_id=1, source_target_pairs={{0,2},{2,4},{4,6},{6,0},{1,3},{3,5},{5,7},{7,1},{8,10},{10,12},{12... | collective-permute-start | bytes 786440 | tf_op jit(solution)/shard_map/ppermute | solution.py:18
  108.4 18.6 %collective-permute-start.15 = (bf16[4,32,1024]{2,1,0:T(8,128)(2,1)}, bf16[4,32,1024]{2,1,0:T(8,128)(2,1)}, u32[]{:S(2)}, u32[]{:S(2)}) collective-permute-start(bf16[4,32,1024]{2,1,0:T(8,128)(2,1)} %bitcast.48), channel_id=1, source_target_pairs={{0,4},{2,6},{4,0},{6,2},{1,5},{3,7},{5,1},{7,3},{8,12},{10,14},{12... | collective-permute-start | bytes 786440 | tf_op jit(solution)/shard_map/ppermute | solution.py:18
  113.0 15.0 %collective-permute-start.16 = (bf16[4,32,1024]{2,1,0:T(8,128)(2,1)}, bf16[4,32,1024]{2,1,0:T(8,128)(2,1)}, u32[]{:S(2)}, u32[]{:S(2)}) collective-permute-start(bf16[4,32,1024]{2,1,0:T(8,128)(2,1)} %bitcast.48), channel_id=1, source_target_pairs={{0,6},{2,0},{4,2},{6,4},{1,7},{3,1},{5,3},{7,5},{8,14},{10,8},{12,... | collective-permute-start | bytes 786440 | tf_op jit(solution)/shard_map/ppermute | solution.py:18
  119.9 18.2 %all-to-all-start.2 = ((bf16[4,64,512]{2,1,0:T(8,128)(2,1)}), bf16[4,64,512]{2,1,0:T(8,128)(2,1)S(1)}, u32[]{:S(2)}, u32[]{:S(2)}) async-start(bf16[4,64,512]{2,1,0:T(8,128)(2,1)} %broadcast_in_dim.104), calls=%async_computation.2 | async-start | bytes 524288 | tf_op jit(solution)/shard_map/all_to_all | solution.py:13
  138.1 31.2 %collective-permute-start.5 = (bf16[256,512]{1,0:T(8,128)(2,1)S(1)}, bf16[256,512]{1,0:T(8,128)(2,1)}, u32[]{:S(2)}, u32[]{:S(2)}) collective-permute-start(bf16[256,512]{1,0:T(8,128)(2,1)S(1)} %bitcast.163), channel_id=1, source_target_pairs={{0,2},{2,4},{4,6},{6,0},{1,3},{3,5},{5,7},{7,1},{8,10},{10,12},{12... | collective-permute-start | bytes 786440 | tf_op jit(solution)/shard_map/ppermute | solution.py:18
  140.0 30.3 %collective-permute-start.6 = (bf16[256,512]{1,0:T(8,128)(2,1)S(1)}, bf16[256,512]{1,0:T(8,128)(2,1)}, u32[]{:S(2)}, u32[]{:S(2)}) collective-permute-start(bf16[256,512]{1,0:T(8,128)(2,1)S(1)} %bitcast.164), channel_id=1, source_target_pairs={{0,4},{2,6},{4,0},{6,2},{1,5},{3,7},{5,1},{7,3},{8,12},{10,14},{12... | collective-permute-start | bytes 786440 | tf_op jit(solution)/shard_map/ppermute | solution.py:18
  145.0 26.3 %collective-permute-start.7 = (bf16[256,512]{1,0:T(8,128)(2,1)S(1)}, bf16[256,512]{1,0:T(8,128)(2,1)S(1)}, u32[]{:S(2)}, u32[]{:S(2)}) collective-permute-start(bf16[256,512]{1,0:T(8,128)(2,1)S(1)} %bitcast.165), channel_id=1, source_target_pairs={{0,6},{2,0},{4,2},{6,4},{1,7},{3,1},{5,3},{7,5},{8,14},{10,8},{12,... | collective-permute-start | bytes 786440 | tf_op jit(solution)/shard_map/ppermute | solution.py:18
  152.0 46.9 %all-to-all-start.4 = ((bf16[256,2,8,128]{3,2,1,0:T(8,128)(2,1)}), bf16[256,2,8,128]{3,2,1,0:T(8,128)(2,1)S(1)}, u32[]{:S(2)}, u32[]{:S(2)}) async-start(bf16[256,2,8,128]{3,2,1,0:T(8,128)(2,1)} %bitcast.57), calls=%async_computation.4 | async-start | bytes 2097152 | tf_op jit(solution)/shard_map/all_to_all | solution.py:13
  169.1 4.1 %copy-start.9 = (s32[32]{0:T(128)S(1)}, s32[32]{0:T(128)}, u32[]{:S(2)}) copy-start(s32[32]{0:T(128)} %param.11) | copy-start | bytes 388
  169.1 4.9 %copy-start.6 = (f32[200]{0:T(256)S(1)}, f32[200]{0:T(256)}, u32[]{:S(2)}) copy-start(f32[200]{0:T(256)} %param.10) | copy-start | bytes 2404
  169.1 9.4 %copy-start.7 = (f32[512]{0:T(512)S(1)}, f32[512]{0:T(512)}, u32[]{:S(2)}) copy-start(f32[512]{0:T(512)} %param.12) | copy-start | bytes 6148
  169.1 9.4 %copy-start.8 = (s32[512]{0:T(512)S(1)}, s32[512]{0:T(512)}, u32[]{:S(2)}) copy-start(s32[512]{0:T(512)} %param.13) | copy-start | bytes 6148
  171.3 8.1 %copy-start.4 = (bf16[4,256,512]{2,1,0:T(8,128)(2,1)}, bf16[4,256,512]{2,1,0:T(8,128)(2,1)S(1)}, u32[]{:S(2)}) copy-start(bf16[4,256,512]{2,1,0:T(8,128)(2,1)S(1)} %bitcast_dynamic-update-slice_fusion.3) | copy-start | bytes 3145732
  171.3 8.1 %collective-permute-start.8 = (bf16[1024,512]{1,0:T(8,128)(2,1)S(1)}, bf16[1024,512]{1,0:T(8,128)(2,1)}, u32[]{:S(2)}, u32[]{:S(2)}) collective-permute-start(bf16[1024,512]{1,0:T(8,128)(2,1)S(1)} %bitcast.167), channel_id=1, source_target_pairs={{0,1},{1,0},{2,3},{3,2},{4,5},{5,4},{6,7},{7,6},{8,9},{9,8},{10,11... | collective-permute-start | bytes 3145736 | tf_op jit(solution)/shard_map/ppermute | solution.py:18
  175.5 3.9 %collective-permute-start.9 = (bf16[512,512]{1,0:T(8,128)(2,1)S(1)}, bf16[512,512]{1,0:T(8,128)(2,1)S(1)}, u32[]{:S(2)}, u32[]{:S(2)}) collective-permute-start(bf16[512,512]{1,0:T(8,128)(2,1)S(1)} %pad_maximum_fusion.1), channel_id=1, source_target_pairs={{0,1},{1,0},{2,3},{3,2},{4,5},{5,4},{6,7},{7,6},{8,9},{9,8},{10,11... | collective-permute-start | bytes 1572872 | tf_op jit(solution)/shard_map/ppermute | solution.py:18
  198.9 1.0 copy-start.3
  198.9 1.3 copy-start.5

commit v4 on v3

--- a/solution.py
+++ b/solution.py
@@ -79,14 +79,16 @@
 
     own = jnp.concatenate([half_of(near, core), half_of(far, core)])
     other = jnp.concatenate([half_of(near, 1 - core), half_of(far, 1 - core)])
+    near_rows = near[:, 16].reshape(8, 1, 2, 1024)
+    far_rows = far[:, 16].reshape(8, 1, 2, 1024)
+    first = lax.axis_index("zl") == 0
+    ladder_rows = jnp.concatenate(
+        [jnp.where(first, near_rows, far_rows), jnp.where(first, far_rows, near_rows)], axis=1
+    ).reshape(32, 1024)
+
     tiles = amplitudes.reshape(2, 64, 8, 4, 128).transpose(1, 3, 0, 2, 4).reshape(256, 2, 8, 128)
     pairs = exchange(tiles, CHIPS)
-    near_rows = gather_ring(near[:, 16].reshape(16, 1024), "zh")
-    far_rows = shifted(near_rows, "zl", 1)
-    first = lax.axis_index("zl") == 0
-    weights = jnp.stack(
-        [jnp.where(first, near_rows, far_rows), jnp.where(first, far_rows, near_rows)], axis=1
-    ).reshape(4, 32, 1024)
+    weights = gather_ring(ladder_rows, "zh")
     weights = gather_ring(weights, "x")
     weights = weights.reshape(512, 1024)
 
@@ -107,7 +109,7 @@
     pairs = pairs.reshape(512, 1024)
     pairs_other = partner(pairs)
     hole = (dot(weights[:, :512], pairs, 1, 0) + dot(weights[:, 512:], pairs_other, 1, 0)).astype(BF)
-    hole = hole.reshape(4, 2, 2, 2, 8, 2, 8, 128).transpose(4, 3, 2, 0, 5, 1, 6, 7).reshape(256, 2, 8, 128)
+    hole = hole.reshape(4, 2, 2, 16, 2, 8, 128).transpose(3, 2, 0, 4, 1, 5, 6).reshape(256, 2, 8, 128)
     hole = exchange(hole, CHIPS)
     hole = hole.reshape(64, 4, 2, 8, 128).transpose(2, 0, 3, 1, 4).reshape(2, VIR, VIR)
 

time: 204 us -> 197 us (0.966)
  starting transfers between devices: 125 us -> 107 us
  waiting for transfers between devices: 40.7 us -> 45.7 us
  local copies, waits for them, and re-layouts: 17.2 us -> 21.6 us
  other arithmetic: 6.64 us -> 9.8 us
    ppermute x18 -> x17, starting transfers between devices: 69.2 us -> 58.8 us  [shifted(): lax.ppermute(value, axis, [(i, (i + step) % count) for i in range(count)])]
    all_to_all x5, starting transfers between devices: 56.3 us -> 48.4 us  [exchange(): return lax.all_to_all(value, axes, split_axis=0, concat_axis=0, tiled=True)]
    dynamic_update_slice x12, local copies, waits for them, and re-layouts: 5.92 us -> 9.24 us  [gather_ring(): lax.dynamic_update_index_in_dim(everyone, near, (me - step) % count, 0)]
    ppermute x18 -> x17, waiting for transfers between devices: 2.04 us -> 4.7 us  [shifted(): lax.ppermute(value, axis, [(i, (i + step) % count) for i in range(count)])]
    all_to_all x5, waiting for transfers between devices: 38.7 us -> 41 us  [exchange(): return lax.all_to_all(value, axes, split_axis=0, concat_axis=0, tiled=True)]
  transfers between devices with their start and end apart: 23 -> 22, of which waited for: 6 -> 6; matrix products, arithmetic and copies ran while one was open for 14% -> 18% of each run, Pallas kernels for 0% -> 0%
where the time goes in v4:
time: 197 us; the launch traced here: 195 us
  starting transfers between devices  107 us (54%)
  waiting for transfers between devices  45.7 us (23%)
  local copies, waits for them, and re-layouts  21.6 us (11%)
  matrix products  9.96 us (5%)
  other arithmetic  9.8 us (5%)
    ppermute x17, starting transfers between devices, shifted(): lax.ppermute(value, axis, [(i, (i + step) % count) for i in range(count)])  58.8 us
    all_to_all x5, starting transfers between devices, exchange(): return lax.all_to_all(value, axes, split_axis=0, concat_axis=0, tiled=True)  48.4 us
    all_to_all x5, waiting for transfers between devices, exchange(): return lax.all_to_all(value, axes, split_axis=0, concat_axis=0, tiled=True)  41 us
    dot_general x7, matrix products, dot(): lax.dot_general(a, b, (((ca,), (cb,)), ((), ())), preferred_element_type=...  9.96 us
    dynamic_update_slice x12, local copies, waits for them, and re-layouts, gather_ring(): lax.dynamic_update_index_in_dim(everyone, near, (me - step) % count, 0)  9.24 us
    ppermute x17, waiting for transfers between devices, shifted(): lax.ppermute(value, axis, [(i, (i + step) % count) for i in range(count)])  4.7 us
  transfers between devices with their start and end apart: 22, of which 6 were waited for; matrix products, arithmetic and copies ran while one was open for 18% of the time, Pallas kernels for 0%

profile of v4, /device:TPU:2, one launch (start us, length us, event | category | flops | bytes accessed | tf_op | source)
XLA Modules:
  0.0 195.0 jit_solution(841661546944337405)
XLA Ops:
  0.0 0.7 copy-done
  0.7 0.7 fusion.5
  1.5 0.9 pad_maximum_fusion.4
  2.3 0.9 broadcast_in_dim.103
  3.2 7.2 %all-to-all-start = ((bf16[16,17,8,128]{3,2,1,0:T(8,128)(2,1)}), bf16[16,17,8,128]{3,2,1,0:T(8,128)(2,1)}, u32[]{:S(2)}, u32[]{:S(2)}) async-start(bf16[16,17,8,128]{3,2,1,0:T(8,128)(2,1)} %bitcast.10), calls=%async_computation | async-start | bytes 1114112 | tf_op jit(solution)/shard_map/all_to_all | solution.py:13
  10.5 0.5 copy.42
  11.0 1.6 broadcast_multiply_fusion
  12.7 14.4 %all-to-all-done = bf16[16,17,8,128]{3,2,1,0:T(8,128)(2,1)} async-done(((bf16[16,17,8,128]{3,2,1,0:T(8,128)(2,1)}), bf16[16,17,8,128]{3,2,1,0:T(8,128)(2,1)}, u32[]{:S(2)}, u32[]{:S(2)}) %all-to-all-start) | async-done | bytes 557088 | tf_op jit(solution)/shard_map/all_to_all | solution.py:13
  27.1 4.3 %collective-permute-start = (bf16[16,17,8,128]{3,2,1,0:T(8,128)(2,1)}, bf16[16,17,8,128]{3,2,1,0:T(8,128)(2,1)}, u32[]{:S(2)}, u32[]{:S(2)}) collective-permute-start(bf16[16,17,8,128]{3,2,1,0:T(8,128)(2,1)} %all-to-all-done), channel_id=1, source_target_pairs={{0,32},{32,0},{1,33},{33,1},{2,34},{34,2},{3,35},{35,3},{4,36},{36... | collective-permute-start | bytes 1671176 | tf_op jit(solution)/shard_map/ppermute | solution.py:18
  31.4 3.0 %fusion.1 = bf16[2,512,512]{2,1,0:T(8,128)(2,1)} fusion(f32[2,512,512]{2,1,0:T(8,128)} %bitcast.140, f32[2,512,512]{1,2,0:T(8,128)S(1)} %copy.42), kind=kLoop, calls=%fused_computation.3 | loop fusion | flops 1048576 | bytes 5242880 | tf_op jit(solution)/shard_map/convert_element_type | solution.py:96
  34.4 3.3 %collective-permute-start.1 = (bf16[1024,512]{1,0:T(8,128)(2,1)}, bf16[1024,512]{1,0:T(8,128)(2,1)S(1)}, u32[]{:S(2)}, u32[]{:S(2)}) collective-permute-start(bf16[1024,512]{1,0:T(8,128)(2,1)} %bitcast.3), channel_id=1, source_target_pairs={{0,1},{1,0},{2,3},{3,2},{4,5},{5,4},{6,7},{7,6},{8,9},{9,8},{10,11... | collective-permute-start | bytes 3145736 | tf_op jit(solution)/shard_map/ppermute | solution.py:18
  37.7 1.3 copy.46
  39.0 16.2 %all-to-all-start.3 = ((bf16[256,2,8,128]{3,2,1,0:T(8,128)(2,1)}), bf16[256,2,8,128]{3,2,1,0:T(8,128)(2,1)S(1)}, u32[]{:S(2)}, u32[]{:S(2)}) async-start(bf16[256,2,8,128]{3,2,1,0:T(8,128)(2,1)} %bitcast.53), calls=%async_computation.3 | async-start | bytes 2097152 | tf_op jit(solution)/shard_map/all_to_all | solution.py:13
  55.4 1.1 dynamic-slice_bitcast_fusion.1
  56.5 0.8 broadcast_select_fusion.1
  57.5 4.3 %collective-permute-start.10 = (bf16[32,1024]{1,0:T(8,128)(2,1)S(1)}, bf16[32,1024]{1,0:T(8,128)(2,1)S(1)}, u32[]{:S(2)}, u32[]{:S(2)}) collective-permute-start(bf16[32,1024]{1,0:T(8,128)(2,1)S(1)} %reshape.276), channel_id=1, source_target_pairs={{0,8},{8,16},{16,24},{24,0},{1,9},{9,17},{17,25},{25,1},{2,10},{10... | collective-permute-start | bytes 196616 | tf_op jit(solution)/shard_map/ppermute | solution.py:18
  61.8 5.5 %collective-permute-start.11 = (bf16[32,1024]{1,0:T(8,128)(2,1)S(1)}, bf16[32,1024]{1,0:T(8,128)(2,1)}, u32[]{:S(2)}, u32[]{:S(2)}) collective-permute-start(bf16[32,1024]{1,0:T(8,128)(2,1)S(1)} %reshape.276), channel_id=1, source_target_pairs={{0,16},{8,24},{16,0},{24,8},{1,17},{9,25},{17,1},{25,9},{2,18},{10... | collective-permute-start | bytes 196616 | tf_op jit(solution)/shard_map/ppermute | solution.py:18
  67.3 1.1 dynamic-slice_bitcast_fusion
  68.5 2.0 %fusion.11 = f32[1024,512]{1,0:T(8,128)S(1)} fusion(bf16[1024,512]{1,0:T(8,128)(2,1)} %bitcast.3, bf16[256,512]{1,0:T(8,128)(2,1)S(1)} %bitcast.154, bf16[256,512]{1,0:T(8,128)(2,1)S(1)} %bitcast.152), kind=kOutput, calls=%fused_computation.23 | convolution fusion | flops 537919488 | bytes 3670016 | tf_op jit(solution)/shard_map/dot_general | solution.py:57
  70.5 0.7 add_convert_fusion.1
  71.4 3.4 %collective-permute-start.2 = (bf16[256,512]{1,0:T(8,128)(2,1)S(1)}, bf16[256,512]{1,0:T(8,128)(2,1)S(1)}, u32[]{:S(2)}, u32[]{:S(2)}) collective-permute-start(bf16[256,512]{1,0:T(8,128)(2,1)S(1)} %get-tuple-element.7), channel_id=1, source_target_pairs={{0,2},{2,4},{4,6},{6,0},{1,3},{3,5},{5,7},{7,1},{8,10},{10,12},{12... | collective-permute-start | bytes 786440 | tf_op jit(solution)/shard_map/ppermute | solution.py:18
  74.7 3.1 %collective-permute-start.3 = (bf16[256,512]{1,0:T(8,128)(2,1)S(1)}, bf16[256,512]{1,0:T(8,128)(2,1)S(1)}, u32[]{:S(2)}, u32[]{:S(2)}) collective-permute-start(bf16[256,512]{1,0:T(8,128)(2,1)S(1)} %get-tuple-element.9), channel_id=1, source_target_pairs={{0,4},{2,6},{4,0},{6,2},{1,5},{3,7},{5,1},{7,3},{8,12},{10,14},{12... | collective-permute-start | bytes 786440 | tf_op jit(solution)/shard_map/ppermute | solution.py:18
  77.8 4.0 %collective-permute-start.4 = (bf16[256,512]{1,0:T(8,128)(2,1)S(1)}, bf16[256,512]{1,0:T(8,128)(2,1)S(1)}, u32[]{:S(2)}, u32[]{:S(2)}) collective-permute-start(bf16[256,512]{1,0:T(8,128)(2,1)S(1)} %get-tuple-element.8), channel_id=1, source_target_pairs={{0,6},{2,0},{4,2},{6,4},{1,7},{3,1},{5,3},{7,5},{8,14},{10,8},{12,... | collective-permute-start | bytes 786440 | tf_op jit(solution)/shard_map/ppermute | solution.py:18
  81.8 0.7 broadcast_in_dim.110
  82.5 0.6 constant_dynamic-update-slice_fusion
  83.2 5.5 %collective-permute-start.12 = (bf16[32,1024]{1,0:T(8,128)(2,1)S(1)}, bf16[32,1024]{1,0:T(8,128)(2,1)S(1)}, u32[]{:S(2)}, u32[]{:S(2)}) collective-permute-start(bf16[32,1024]{1,0:T(8,128)(2,1)S(1)} %reshape.276), channel_id=1, source_target_pairs={{0,24},{8,0},{16,8},{24,16},{1,25},{9,1},{17,9},{25,17},{2,26},{10... | collective-permute-start | bytes 196616 | tf_op jit(solution)/shard_map/ppermute | solution.py:18
  88.6 0.6 bitcast_dynamic-update-slice_fusion.10
  89.3 3.6 %collective-permute-done.4 = bf16[256,512]{1,0:T(8,128)(2,1)S(1)} collective-permute-done((bf16[256,512]{1,0:T(8,128)(2,1)S(1)}, bf16[256,512]{1,0:T(8,128)(2,1)S(1)}, u32[]{:S(2)}, u32[]{:S(2)}) %collective-permute-start.4) | collective-permute-done | bytes 262176 | tf_op jit(solution)/shard_map/ppermute | solution.py:18
  92.9 0.9 fusion.10
  93.8 4.1 %all-to-all-start.1 = ((f32[4,64,512]{2,1,0:T(8,128)}), f32[4,64,512]{2,1,0:T(8,128)S(1)}, u32[]{:S(2)}, u32[]{:S(2)}) async-start(f32[4,64,512]{2,1,0:T(8,128)} %bitcast.34), calls=%async_computation.1 | async-start | bytes 1048576 | tf_op jit(solution)/shard_map/all_to_all | solution.py:13
  97.9 1.5 bitcast_dynamic-update-slice_fusion.9
  99.4 1.2 copy.56
  100.6 1.9 collective-permute-start.16
  102.6 0.6 bitcast_dynamic-update-slice_fusion.8
  103.2 2.5 %collective-permute-start.13 = (bf16[4,32,1024]{2,1,0:T(8,128)(2,1)}, bf16[4,32,1024]{2,1,0:T(8,128)(2,1)}, u32[]{:S(2)}, u32[]{:S(2)}) collective-permute-start(bf16[4,32,1024]{2,1,0:T(8,128)(2,1)} %bitcast_dynamic-update-slice_fusion.8), channel_id=1, source_target_pairs={{0,2},{2,4},{4,6},{6,0},{1,3},{3,5},{5,7},{7,1},{8,10},{10,12},{12... | collective-permute-start | bytes 786440 | tf_op jit(solution)/shard_map/ppermute | solution.py:18
  105.8 3.3 %collective-permute-start.14 = (bf16[4,32,1024]{2,1,0:T(8,128)(2,1)}, bf16[4,32,1024]{2,1,0:T(8,128)(2,1)}, u32[]{:S(2)}, u32[]{:S(2)}) collective-permute-start(bf16[4,32,1024]{2,1,0:T(8,128)(2,1)} %bitcast_dynamic-update-slice_fusion.8), channel_id=1, source_target_pairs={{0,4},{2,6},{4,0},{6,2},{1,5},{3,7},{5,1},{7,3},{8,12},{10,14},{12... | collective-permute-start | bytes 786440 | tf_op jit(solution)/shard_map/ppermute | solution.py:18
  109.1 3.9 %collective-permute-start.15 = (bf16[4,32,1024]{2,1,0:T(8,128)(2,1)}, bf16[4,32,1024]{2,1,0:T(8,128)(2,1)}, u32[]{:S(2)}, u32[]{:S(2)}) collective-permute-start(bf16[4,32,1024]{2,1,0:T(8,128)(2,1)} %bitcast_dynamic-update-slice_fusion.8), channel_id=1, source_target_pairs={{0,6},{2,0},{4,2},{6,4},{1,7},{3,1},{5,3},{7,5},{8,14},{10,8},{12,... | collective-permute-start | bytes 786440 | tf_op jit(solution)/shard_map/ppermute | solution.py:18
  113.1 1.0 bitcast_dynamic-update-slice_fusion.3
  114.1 0.5 collective-permute-done.13
  114.6 1.0 bitcast_dynamic-update-slice_fusion.2
  115.6 0.7 broadcast_in_dim.104
  116.3 7.2 %all-to-all-start.2 = ((bf16[4,64,512]{2,1,0:T(8,128)(2,1)}), bf16[4,64,512]{2,1,0:T(8,128)(2,1)S(1)}, u32[]{:S(2)}, u32[]{:S(2)}) async-start(bf16[4,64,512]{2,1,0:T(8,128)(2,1)} %broadcast_in_dim.104), calls=%async_computation.2 | async-start | bytes 524288 | tf_op jit(solution)/shard_map/all_to_all | solution.py:13
  123.5 1.0 bitcast_dynamic-update-slice_fusion.1
  124.5 1.0 bitcast_dynamic-update-slice_fusion
  125.5 8.2 %all-to-all-done.2 = bf16[4,64,512]{2,1,0:T(8,128)(2,1)S(1)} async-done(((bf16[4,64,512]{2,1,0:T(8,128)(2,1)}), bf16[4,64,512]{2,1,0:T(8,128)(2,1)S(1)}, u32[]{:S(2)}, u32[]{:S(2)}) %all-to-all-start.2) | async-done | bytes 262176 | tf_op jit(solution)/shard_map/all_to_all | solution.py:13
  133.7 2.6 %collective-permute-start.5 = (bf16[256,512]{1,0:T(8,128)(2,1)S(1)}, bf16[256,512]{1,0:T(8,128)(2,1)}, u32[]{:S(2)}, u32[]{:S(2)}) collective-permute-start(bf16[256,512]{1,0:T(8,128)(2,1)S(1)} %bitcast.156), channel_id=1, source_target_pairs={{0,2},{2,4},{4,6},{6,0},{1,3},{3,5},{5,7},{7,1},{8,10},{10,12},{12... | collective-permute-start | bytes 786440 | tf_op jit(solution)/shard_map/ppermute | solution.py:18
  136.2 4.7 %collective-permute-start.6 = (bf16[256,512]{1,0:T(8,128)(2,1)S(1)}, bf16[256,512]{1,0:T(8,128)(2,1)}, u32[]{:S(2)}, u32[]{:S(2)}) collective-permute-start(bf16[256,512]{1,0:T(8,128)(2,1)S(1)} %bitcast.157), channel_id=1, source_target_pairs={{0,4},{2,6},{4,0},{6,2},{1,5},{3,7},{5,1},{7,3},{8,12},{10,14},{12... | collective-permute-start | bytes 786440 | tf_op jit(solution)/shard_map/ppermute | solution.py:18
  140.9 2.3 %collective-permute-start.7 = (bf16[256,512]{1,0:T(8,128)(2,1)S(1)}, bf16[256,512]{1,0:T(8,128)(2,1)S(1)}, u32[]{:S(2)}, u32[]{:S(2)}) collective-permute-start(bf16[256,512]{1,0:T(8,128)(2,1)S(1)} %bitcast.158), channel_id=1, source_target_pairs={{0,6},{2,0},{4,2},{6,4},{1,7},{3,1},{5,3},{7,5},{8,14},{10,8},{12,... | collective-permute-start | bytes 786440 | tf_op jit(solution)/shard_map/ppermute | solution.py:18
  143.3 1.9 fusion.6
  145.2 0.7 fusion.3
  146.2 1.3 copy.47
  147.5 13.7 %all-to-all-start.4 = ((bf16[256,2,8,128]{3,2,1,0:T(8,128)(2,1)}), bf16[256,2,8,128]{3,2,1,0:T(8,128)(2,1)S(1)}, u32[]{:S(2)}, u32[]{:S(2)}) async-start(bf16[256,2,8,128]{3,2,1,0:T(8,128)(2,1)} %bitcast.55), calls=%async_computation.4 | async-start | bytes 2097152 | tf_op jit(solution)/shard_map/all_to_all | solution.py:13
  161.3 1.0 bitcast_dynamic-update-slice_fusion.6
  162.3 1.0 bitcast_dynamic-update-slice_fusion.5
  163.4 1.9 collective-permute-start.8
  165.3 0.7 dynamic_slice.41
  166.1 1.3 fusion.32
  167.6 2.4 %collective-permute-start.9 = (bf16[512,512]{1,0:T(8,128)(2,1)S(1)}, bf16[512,512]{1,0:T(8,128)(2,1)S(1)}, u32[]{:S(2)}, u32[]{:S(2)}) collective-permute-start(bf16[512,512]{1,0:T(8,128)(2,1)S(1)} %pad_maximum_fusion.1), channel_id=1, source_target_pairs={{0,1},{1,0},{2,3},{3,2},{4,5},{5,4},{6,7},{7,6},{8,9},{9,8},{10,11... | collective-permute-start | bytes 1572872 | tf_op jit(solution)/shard_map/ppermute | solution.py:18
  170.0 0.6 broadcast_add_fusion
  171.0 0.5 collective-permute-done.9
  171.5 1.9 fusion.36
  173.4 18.4 %all-to-all-done.4 = bf16[256,2,8,128]{3,2,1,0:T(8,128)(2,1)S(1)} async-done(((bf16[256,2,8,128]{3,2,1,0:T(8,128)(2,1)}), bf16[256,2,8,128]{3,2,1,0:T(8,128)(2,1)S(1)}, u32[]{:S(2)}, u32[]{:S(2)}) %all-to-all-start.4) | async-done | bytes 1048608 | tf_op jit(solution)/shard_map/all_to_all | solution.py:13
  192.1 0.7 copy-done.3
  193.2 1.8 divide_convert_fusion
  (63 shorter events, 2.2 us)
Async XLA Ops:
  0.0 0.7 copy-start
  0.0 10.5 %copy-start.1 = (bf16[1024,512]{1,0:T(8,128)(2,1)S(1)}, bf16[1024,512]{1,0:T(8,128)(2,1)}, u32[]{:S(2)}) copy-start(bf16[1024,512]{1,0:T(8,128)(2,1)} %param.7) | copy-start | bytes 3145732
  3.2 23.9 %all-to-all-start = ((bf16[16,17,8,128]{3,2,1,0:T(8,128)(2,1)}), bf16[16,17,8,128]{3,2,1,0:T(8,128)(2,1)}, u32[]{:S(2)}, u32[]{:S(2)}) async-start(bf16[16,17,8,128]{3,2,1,0:T(8,128)(2,1)} %bitcast.10), calls=%async_computation | async-start | bytes 1114112 | tf_op jit(solution)/shard_map/all_to_all | solution.py:13
  27.1 29.4 %collective-permute-start = (bf16[16,17,8,128]{3,2,1,0:T(8,128)(2,1)}, bf16[16,17,8,128]{3,2,1,0:T(8,128)(2,1)}, u32[]{:S(2)}, u32[]{:S(2)}) collective-permute-start(bf16[16,17,8,128]{3,2,1,0:T(8,128)(2,1)} %all-to-all-done), channel_id=1, source_target_pairs={{0,32},{32,0},{1,33},{33,1},{2,34},{34,2},{3,35},{35,3},{4,36},{36... | collective-permute-start | bytes 1671176 | tf_op jit(solution)/shard_map/ppermute | solution.py:18
  34.4 36.2 %collective-permute-start.1 = (bf16[1024,512]{1,0:T(8,128)(2,1)}, bf16[1024,512]{1,0:T(8,128)(2,1)S(1)}, u32[]{:S(2)}, u32[]{:S(2)}) collective-permute-start(bf16[1024,512]{1,0:T(8,128)(2,1)} %bitcast.3), channel_id=1, source_target_pairs={{0,1},{1,0},{2,3},{3,2},{4,5},{5,4},{6,7},{7,6},{8,9},{9,8},{10,11... | collective-permute-start | bytes 3145736 | tf_op jit(solution)/shard_map/ppermute | solution.py:18
  39.0 54.9 %all-to-all-start.3 = ((bf16[256,2,8,128]{3,2,1,0:T(8,128)(2,1)}), bf16[256,2,8,128]{3,2,1,0:T(8,128)(2,1)S(1)}, u32[]{:S(2)}, u32[]{:S(2)}) async-start(bf16[256,2,8,128]{3,2,1,0:T(8,128)(2,1)} %bitcast.53), calls=%async_computation.3 | async-start | bytes 2097152 | tf_op jit(solution)/shard_map/all_to_all | solution.py:13
  57.5 25.6 %collective-permute-start.10 = (bf16[32,1024]{1,0:T(8,128)(2,1)S(1)}, bf16[32,1024]{1,0:T(8,128)(2,1)S(1)}, u32[]{:S(2)}, u32[]{:S(2)}) collective-permute-start(bf16[32,1024]{1,0:T(8,128)(2,1)S(1)} %reshape.276), channel_id=1, source_target_pairs={{0,8},{8,16},{16,24},{24,0},{1,9},{9,17},{17,25},{25,1},{2,10},{10... | collective-permute-start | bytes 196616 | tf_op jit(solution)/shard_map/ppermute | solution.py:18
  61.8 36.1 %collective-permute-start.11 = (bf16[32,1024]{1,0:T(8,128)(2,1)S(1)}, bf16[32,1024]{1,0:T(8,128)(2,1)}, u32[]{:S(2)}, u32[]{:S(2)}) collective-permute-start(bf16[32,1024]{1,0:T(8,128)(2,1)S(1)} %reshape.276), channel_id=1, source_target_pairs={{0,16},{8,24},{16,0},{24,8},{1,17},{9,25},{17,1},{25,9},{2,18},{10... | collective-permute-start | bytes 196616 | tf_op jit(solution)/shard_map/ppermute | solution.py:18
  68.4 2.1 %copy-start.2 = (bf16[8,16,8,128]{3,2,1,0:T(8,128)(2,1)}, bf16[8,16,8,128]{3,2,1,0:T(8,128)(2,1)S(1)}, u32[]{:S(2)}) copy-start(bf16[8,16,8,128]{3,2,1,0:T(8,128)(2,1)S(1)} %slice.48) | copy-start | bytes 786436
  71.4 17.9 %collective-permute-start.2 = (bf16[256,512]{1,0:T(8,128)(2,1)S(1)}, bf16[256,512]{1,0:T(8,128)(2,1)S(1)}, u32[]{:S(2)}, u32[]{:S(2)}) collective-permute-start(bf16[256,512]{1,0:T(8,128)(2,1)S(1)} %get-tuple-element.7), channel_id=1, source_target_pairs={{0,2},{2,4},{4,6},{6,0},{1,3},{3,5},{5,7},{7,1},{8,10},{10,12},{12... | collective-permute-start | bytes 786440 | tf_op jit(solution)/shard_map/ppermute | solution.py:18
  74.7 14.5 %collective-permute-start.3 = (bf16[256,512]{1,0:T(8,128)(2,1)S(1)}, bf16[256,512]{1,0:T(8,128)(2,1)S(1)}, u32[]{:S(2)}, u32[]{:S(2)}) collective-permute-start(bf16[256,512]{1,0:T(8,128)(2,1)S(1)} %get-tuple-element.9), channel_id=1, source_target_pairs={{0,4},{2,6},{4,0},{6,2},{1,5},{3,7},{5,1},{7,3},{8,12},{10,14},{12... | collective-permute-start | bytes 786440 | tf_op jit(solution)/shard_map/ppermute | solution.py:18
  77.8 15.1 %collective-permute-start.4 = (bf16[256,512]{1,0:T(8,128)(2,1)S(1)}, bf16[256,512]{1,0:T(8,128)(2,1)S(1)}, u32[]{:S(2)}, u32[]{:S(2)}) collective-permute-start(bf16[256,512]{1,0:T(8,128)(2,1)S(1)} %get-tuple-element.8), channel_id=1, source_target_pairs={{0,6},{2,0},{4,2},{6,4},{1,7},{3,1},{5,3},{7,5},{8,14},{10,8},{12,... | collective-permute-start | bytes 786440 | tf_op jit(solution)/shard_map/ppermute | solution.py:18
  83.2 19.4 %collective-permute-start.12 = (bf16[32,1024]{1,0:T(8,128)(2,1)S(1)}, bf16[32,1024]{1,0:T(8,128)(2,1)S(1)}, u32[]{:S(2)}, u32[]{:S(2)}) collective-permute-start(bf16[32,1024]{1,0:T(8,128)(2,1)S(1)} %reshape.276), channel_id=1, source_target_pairs={{0,24},{8,0},{16,8},{24,16},{1,25},{9,1},{17,9},{25,17},{2,26},{10... | collective-permute-start | bytes 196616 | tf_op jit(solution)/shard_map/ppermute | solution.py:18
  93.8 21.7 %all-to-all-start.1 = ((f32[4,64,512]{2,1,0:T(8,128)}), f32[4,64,512]{2,1,0:T(8,128)S(1)}, u32[]{:S(2)}, u32[]{:S(2)}) async-start(f32[4,64,512]{2,1,0:T(8,128)} %bitcast.34), calls=%async_computation.1 | async-start | bytes 1048576 | tf_op jit(solution)/shard_map/all_to_all | solution.py:13
  100.6 42.6 %collective-permute-start.16 = (bf16[512,1024]{1,0:T(8,128)(2,1)}, bf16[512,1024]{1,0:T(8,128)(2,1)}, u32[]{:S(2)}, u32[]{:S(2)}) collective-permute-start(bf16[512,1024]{1,0:T(8,128)(2,1)} %bitcast.131), channel_id=1, source_target_pairs={{0,1},{1,0},{2,3},{3,2},{4,5},{5,4},{6,7},{7,6},{8,9},{9,8},{10,11... | collective-permute-start | bytes 3145736 | tf_op jit(solution)/shard_map/ppermute | solution.py:18
  103.2 11.4 %collective-permute-start.13 = (bf16[4,32,1024]{2,1,0:T(8,128)(2,1)}, bf16[4,32,1024]{2,1,0:T(8,128)(2,1)}, u32[]{:S(2)}, u32[]{:S(2)}) collective-permute-start(bf16[4,32,1024]{2,1,0:T(8,128)(2,1)} %bitcast_dynamic-update-slice_fusion.8), channel_id=1, source_target_pairs={{0,2},{2,4},{4,6},{6,0},{1,3},{3,5},{5,7},{7,1},{8,10},{10,12},{12... | collective-permute-start | bytes 786440 | tf_op jit(solution)/shard_map/ppermute | solution.py:18
  105.8 17.8 %collective-permute-start.14 = (bf16[4,32,1024]{2,1,0:T(8,128)(2,1)}, bf16[4,32,1024]{2,1,0:T(8,128)(2,1)}, u32[]{:S(2)}, u32[]{:S(2)}) collective-permute-start(bf16[4,32,1024]{2,1,0:T(8,128)(2,1)} %bitcast_dynamic-update-slice_fusion.8), channel_id=1, source_target_pairs={{0,4},{2,6},{4,0},{6,2},{1,5},{3,7},{5,1},{7,3},{8,12},{10,14},{12... | collective-permute-start | bytes 786440 | tf_op jit(solution)/shard_map/ppermute | solution.py:18
  109.1 15.5 %collective-permute-start.15 = (bf16[4,32,1024]{2,1,0:T(8,128)(2,1)}, bf16[4,32,1024]{2,1,0:T(8,128)(2,1)}, u32[]{:S(2)}, u32[]{:S(2)}) collective-permute-start(bf16[4,32,1024]{2,1,0:T(8,128)(2,1)} %bitcast_dynamic-update-slice_fusion.8), channel_id=1, source_target_pairs={{0,6},{2,0},{4,2},{6,4},{1,7},{3,1},{5,3},{7,5},{8,14},{10,8},{12,... | collective-permute-start | bytes 786440 | tf_op jit(solution)/shard_map/ppermute | solution.py:18
  116.3 17.3 %all-to-all-start.2 = ((bf16[4,64,512]{2,1,0:T(8,128)(2,1)}), bf16[4,64,512]{2,1,0:T(8,128)(2,1)S(1)}, u32[]{:S(2)}, u32[]{:S(2)}) async-start(bf16[4,64,512]{2,1,0:T(8,128)(2,1)} %broadcast_in_dim.104), calls=%async_computation.2 | async-start | bytes 524288 | tf_op jit(solution)/shard_map/all_to_all | solution.py:13
  133.7 27.7 %collective-permute-start.5 = (bf16[256,512]{1,0:T(8,128)(2,1)S(1)}, bf16[256,512]{1,0:T(8,128)(2,1)}, u32[]{:S(2)}, u32[]{:S(2)}) collective-permute-start(bf16[256,512]{1,0:T(8,128)(2,1)S(1)} %bitcast.156), channel_id=1, source_target_pairs={{0,2},{2,4},{4,6},{6,0},{1,3},{3,5},{5,7},{7,1},{8,10},{10,12},{12... | collective-permute-start | bytes 786440 | tf_op jit(solution)/shard_map/ppermute | solution.py:18
  136.2 26.1 %collective-permute-start.6 = (bf16[256,512]{1,0:T(8,128)(2,1)S(1)}, bf16[256,512]{1,0:T(8,128)(2,1)}, u32[]{:S(2)}, u32[]{:S(2)}) collective-permute-start(bf16[256,512]{1,0:T(8,128)(2,1)S(1)} %bitcast.157), channel_id=1, source_target_pairs={{0,4},{2,6},{4,0},{6,2},{1,5},{3,7},{5,1},{7,3},{8,12},{10,14},{12... | collective-permute-start | bytes 786440 | tf_op jit(solution)/shard_map/ppermute | solution.py:18
  140.9 22.4 %collective-permute-start.7 = (bf16[256,512]{1,0:T(8,128)(2,1)S(1)}, bf16[256,512]{1,0:T(8,128)(2,1)S(1)}, u32[]{:S(2)}, u32[]{:S(2)}) collective-permute-start(bf16[256,512]{1,0:T(8,128)(2,1)S(1)} %bitcast.158), channel_id=1, source_target_pairs={{0,6},{2,0},{4,2},{6,4},{1,7},{3,1},{5,3},{7,5},{8,14},{10,8},{12,... | collective-permute-start | bytes 786440 | tf_op jit(solution)/shard_map/ppermute | solution.py:18
  147.5 44.4 %all-to-all-start.4 = ((bf16[256,2,8,128]{3,2,1,0:T(8,128)(2,1)}), bf16[256,2,8,128]{3,2,1,0:T(8,128)(2,1)S(1)}, u32[]{:S(2)}, u32[]{:S(2)}) async-start(bf16[256,2,8,128]{3,2,1,0:T(8,128)(2,1)} %bitcast.55), calls=%async_computation.4 | async-start | bytes 2097152 | tf_op jit(solution)/shard_map/all_to_all | solution.py:13
  161.2 4.1 %copy-start.9 = (s32[32]{0:T(128)S(1)}, s32[32]{0:T(128)}, u32[]{:S(2)}) copy-start(s32[32]{0:T(128)} %param.11) | copy-start | bytes 388
  161.2 4.9 %copy-start.6 = (f32[200]{0:T(256)S(1)}, f32[200]{0:T(256)}, u32[]{:S(2)}) copy-start(f32[200]{0:T(256)} %param.10) | copy-start | bytes 2404
  161.2 9.5 %copy-start.7 = (f32[512]{0:T(512)S(1)}, f32[512]{0:T(512)}, u32[]{:S(2)}) copy-start(f32[512]{0:T(512)} %param.12) | copy-start | bytes 6148
  161.2 9.5 %copy-start.8 = (s32[512]{0:T(512)S(1)}, s32[512]{0:T(512)}, u32[]{:S(2)}) copy-start(s32[512]{0:T(512)} %param.13) | copy-start | bytes 6148
  163.3 8.2 %copy-start.4 = (bf16[4,256,512]{2,1,0:T(8,128)(2,1)}, bf16[4,256,512]{2,1,0:T(8,128)(2,1)S(1)}, u32[]{:S(2)}) copy-start(bf16[4,256,512]{2,1,0:T(8,128)(2,1)S(1)} %bitcast_dynamic-update-slice_fusion.4) | copy-start | bytes 3145732
  163.4 8.2 %collective-permute-start.8 = (bf16[1024,512]{1,0:T(8,128)(2,1)S(1)}, bf16[1024,512]{1,0:T(8,128)(2,1)}, u32[]{:S(2)}, u32[]{:S(2)}) collective-permute-start(bf16[1024,512]{1,0:T(8,128)(2,1)S(1)} %bitcast.160), channel_id=1, source_target_pairs={{0,1},{1,0},{2,3},{3,2},{4,5},{5,4},{6,7},{7,6},{8,9},{9,8},{10,11... | collective-permute-start | bytes 3145736 | tf_op jit(solution)/shard_map/ppermute | solution.py:18
  167.6 3.9 %collective-permute-start.9 = (bf16[512,512]{1,0:T(8,128)(2,1)S(1)}, bf16[512,512]{1,0:T(8,128)(2,1)S(1)}, u32[]{:S(2)}, u32[]{:S(2)}) collective-permute-start(bf16[512,512]{1,0:T(8,128)(2,1)S(1)} %pad_maximum_fusion.1), channel_id=1, source_target_pairs={{0,1},{1,0},{2,3},{3,2},{4,5},{5,4},{6,7},{7,6},{8,9},{9,8},{10,11... | collective-permute-start | bytes 1572872 | tf_op jit(solution)/shard_map/ppermute | solution.py:18
  191.9 1.0 copy-start.3
  191.9 1.3 copy-start.5
